TPU v7x, 128 devices: a whole 4x4x4 slice. The times are simulated.
128 devices in a mesh: obs: 16 (over z, y), lvl: 8 (over x, core).
Axes of the slice: x: 4, y: 4, z: 4, core: 2. Of those that a mesh axis runs over, the one named last changes fastest.
Arguments:
- rhs: float32 [64, 1048576], P(None, ('obs', 'lvl')), may hold values from -15 to 15
- tile_weights: bfloat16 [16384, 64, 128], P(('obs', 'lvl')), may hold values from -0.3125 to 0.3125
- tile_owner: int32 [16384, 1], P(('obs', 'lvl')), may hold values from 0 to 127; in each aligned block of 128 rows (0 to 127, 128 to 255, ...) at most 2 rows name the same one
- tile_row: int32 [16384], P(('obs', 'lvl')), may hold values from 0 to 7
- axis_a: bfloat16 [128, 8, 128], P('obs', 'lvl'), as said below
- axis_b: bfloat16 [8, 128, 128], P('lvl'), as said below
- coupling: float32 [8, 8], replicated, as said below
- noise: float32 [64], replicated, may hold values from 0.1 to 1
Outputs:
- solution: float32 [64, 1048576], P(None, ('obs', 'lvl'))
- residual: float32 [64, 1048576], P(None, ('obs', 'lvl'))
Inputs may be any that keep to these rules, and one draw needn't show every extreme that they name: `tile_owner`: among the 128 tiles of one device no owner is named more than 2 times, a bound that some block reaches. For each level l, axis_a[x, l, a] equals axis_a[a, l, x]. For each level l, axis_b[l] is symmetric. coupling is symmetric and positive definite.
All inputs are finite; a program needn't handle non-finite values.
Results may differ from a plain program's by a relative error of at most 0.017.
Values may be sent and summed in bfloat16 or wider, within the bound.
A program may use at most 64 MiB of HBM per device.

v0:
```python
import functools

import jax
import jax.numpy as jnp
from jax import lax
from jax.sharding import Mesh
from jax.sharding import PartitionSpec as P

ITERS = 2
OBS_LVL = ("obs_0", "obs_1", "lvl_0", "lvl_1")
OBS = ("obs_0", "obs_1")
LVL = ("lvl_0", "lvl_1")


def joined_along(pieces, dim):
    dims = list(pieces.shape[1:])
    dims[dim] *= pieces.shape[0]
    return jnp.moveaxis(pieces, 0, dim).reshape(dims)


def from_everyone(shard, axis):
    copies = jnp.broadcast_to(shard, (lax.axis_size(axis), *shard.shape))
    return lax.all_to_all(copies, axis, split_axis=0, concat_axis=0, tiled=True)


def gathered_copies(shard, axis, dim):
    return joined_along(from_everyone(shard, axis), dim)


def by_axis(shard, axes):
    return functools.reduce(lax.psum, axes, shard)


def on_device(rhs, tile_weights, tile_owner, tile_row, axis_a, axis_b, coupling, noise):
    devices = lax.axis_size(OBS_LVL)
    obs_count = lax.axis_size(OBS)
    lvl_count = lax.axis_size(LVL)
    tile_count, tile_obs, node_cols = tile_weights.shape
    columns = rhs.shape[0]
    a_rows, lvl_here, grid_first = axis_a.shape
    capacity = max(2, 2 * tile_count // devices)
    owner = tile_owner[:, 0]
    my_coupling = lax.dynamic_slice_in_dim(coupling, lax.axis_index(LVL) * lvl_here, lvl_here, 0)
    col_width = columns // obs_count
    lvl_cap = obs_count * capacity
    lvl_slots = lvl_count * lvl_cap
    whole_rows = grid_first * lvl_here
    whole_kernel = gathered_copies(axis_a, OBS, 0)
    level_of = owner % lvl_count
    lvl_hits = (level_of[:, None] == jnp.arange(lvl_count, dtype=jnp.int32)[None, :]).astype(
        jnp.int32
    )
    lvl_before = jnp.cumsum(lvl_hits, axis=0) - lvl_hits
    lvl_position = jnp.sum(lvl_before * lvl_hits, axis=1)
    lvl_slot = level_of * lvl_cap + lvl_position
    first_index = owner // lvl_count * a_rows + tile_row // lvl_here
    target = first_index * lvl_here + tile_row % lvl_here
    target_out = jnp.zeros((lvl_slots,), jnp.int32).at[lvl_slot].set(target)
    target_out = jnp.broadcast_to(target_out[None, :], (obs_count, lvl_slots)).reshape(
        devices, lvl_cap
    )
    col_rows = lax.all_to_all(target_out, OBS_LVL, split_axis=0, concat_axis=0, tiled=True).reshape(
        devices * lvl_cap
    )
    col_collect = (jnp.arange(whole_rows, dtype=jnp.int32)[:, None] == col_rows[None, :]).astype(
        jnp.bfloat16
    )

    def local_axes(field):
        first = jnp.einsum(
            "alrb,lbc->alrc", field, axis_b, preferred_element_type=jnp.float32
        ).astype(jnp.bfloat16)
        return jnp.einsum(
            "xla,alrc->xlrc", whole_kernel, first, preferred_element_type=jnp.float32
        ).astype(jnp.bfloat16)

    def squared_norm(field):
        return by_axis(jnp.sum(field * field, axis=1), OBS_LVL)

    solution = jnp.zeros_like(rhs)
    residual = rhs
    direction = rhs
    norm_now = squared_norm(residual)
    for step in range(ITERS):
        low = direction.astype(jnp.bfloat16).reshape(obs_count, col_width, tile_count, tile_obs)
        part = jnp.einsum(
            "jckt,ktn->jkcn", low, tile_weights, preferred_element_type=jnp.float32
        ).astype(jnp.bfloat16)
        outgoing = (
            jnp.zeros((obs_count, lvl_slots, col_width, node_cols), jnp.bfloat16)
            .at[:, lvl_slot]
            .set(part)
        )
        outgoing = outgoing.reshape(devices, lvl_cap, col_width, node_cols)
        received = lax.all_to_all(outgoing, OBS_LVL, split_axis=0, concat_axis=0, tiled=True)
        width = received.shape[2]
        flat = received.reshape(devices * lvl_cap, width * node_cols)
        summed = jnp.dot(col_collect, flat, preferred_element_type=jnp.float32)
        node_sums = summed.reshape(whole_rows, width, node_cols).astype(jnp.bfloat16)
        grid = node_sums.reshape(grid_first, lvl_here, col_width, node_cols)
        grid_values = local_axes(
            jnp.einsum(
                "lm,amrc->alrc",
                my_coupling,
                gathered_copies(local_axes(grid), LVL, 1).astype(jnp.float32),
                precision=lax.Precision.HIGHEST,
            ).astype(jnp.bfloat16)
        ).reshape(whole_rows, col_width, node_cols)
        returning = grid_values[col_rows].reshape(devices, lvl_cap, col_width, node_cols)
        spread_received = lax.all_to_all(
            returning, OBS_LVL, split_axis=0, concat_axis=0, tiled=True
        )
        spread_width = spread_received.shape[2]
        mine = spread_received.reshape(obs_count, lvl_slots, spread_width, node_cols)[:, lvl_slot]
        values = jnp.einsum(
            "jkcn,ktn->jckt", mine, tile_weights, preferred_element_type=jnp.float32
        )
        back = values.astype(jnp.bfloat16).reshape(obs_count, spread_width, tile_count * tile_obs)
        back = back.reshape(columns, tile_count * tile_obs)
        image = back.astype(jnp.float32) + noise[:, None] * direction
        alpha = norm_now / by_axis(jnp.sum(direction * image, axis=1), OBS_LVL)
        solution = solution + alpha[:, None] * direction
        residual = residual - alpha[:, None] * image
        if step + 1 < ITERS:
            norm_next = squared_norm(residual)
            direction = residual + (norm_next / norm_now)[:, None] * direction
            norm_now = norm_next
    return (solution, residual)


def solution(mesh):
    split = Mesh(mesh.devices.reshape(4, 4, 4, 2), ("obs_0", "obs_1", "lvl_0", "lvl_1"))
    in_specs = (
        P(None, OBS_LVL),
        P(OBS_LVL, None, None),
        P(OBS_LVL, None),
        P(OBS_LVL),
        P(OBS, LVL, None),
        P(LVL, None, None),
        P(),
        P(),
    )
    out_specs = (P(None, OBS_LVL), P(None, OBS_LVL))
    return jax.shard_map(
        on_device, mesh=split, in_specs=in_specs, out_specs=out_specs, check_vma=False
    )
```

profile of v0, /device:TPU:1, one launch (start us, length us, event | category | flops | bytes accessed | tf_op | source)
XLA Modules:
  0.0 629.9 jit_solution(6862280522562374841)
XLA Ops:
  5.0 11.5 %all-to-all-start = ((s32[128,1,32]{2,1,0:T(1,128)}), s32[128,1,32]{2,1,0:T(1,128)S(1)}, u32[]{:S(2)}, u32[]{:S(2)}) async-start(s32[128,1,32]{2,1,0:T(1,128)} %bitcast.4), calls=%async_computation | async-start | bytes 131072 | tf_op jit(solution)/shard_map/all_to_all | solution.py:62
  28.9 17.6 %scatter_fusion = bf16[16,256,4,128]{3,0,2,1:T(8,128)(2,1)} fusion(bf16[16,256,4,128]{3,0,2,1:T(8,128)(2,1)} %broadcast.85.clone, s32[128]{0:T(128)S(1)} %fusion.68, bf16[128,16,4,128]{3,1,2,0:T(8,128)(2,1)} %convert_bitcast_fusion.2), kind=kCustom, calls=%fused_computation.5 | custom fusion | bytes 6291968 | tf_op jit(solution)/shard_map/scatter | solution.py:92
  54.7 10.2 %all-to-all-start.1 = ((bf16[128,32,4,128]{3,1,2,0:T(8,128)(2,1)}), bf16[128,32,4,128]{3,1,2,0:T(8,128)(2,1)}, u32[]{:S(2)}, u32[]{:S(2)}) async-start(bf16[128,32,4,128]{3,1,2,0:T(8,128)(2,1)} %copy.52), calls=%async_computation.1 | async-start | bytes 8388608 | tf_op jit(solution)/shard_map/all_to_all | solution.py:95
  66.4 51.1 %all-to-all-done.1 = bf16[128,32,4,128]{3,1,2,0:T(8,128)(2,1)} async-done(((bf16[128,32,4,128]{3,1,2,0:T(8,128)(2,1)}), bf16[128,32,4,128]{3,1,2,0:T(8,128)(2,1)}, u32[]{:S(2)}, u32[]{:S(2)}) %all-to-all-start.1) | async-done | bytes 4194336 | tf_op jit(solution)/shard_map/all_to_all | solution.py:95
  130.9 6.5 %copy.54 = bf16[512,4096]{1,0:T(8,128)(2,1)} copy(bf16[512,4096]{0,1:T(8,128)(2,1)} %bitcast.179) | data formatting | bytes 8388608 | tf_op jit(solution)/shard_map/dot_general | solution.py:98
  147.3 15.0 %all-to-all-done.3 = bf16[8,128,1,4,128]{4,3,2,1,0:T(4,128)(2,1)S(1)} async-done(((bf16[8,128,1,4,128]{4,3,2,1,0:T(4,128)(2,1)}), bf16[8,128,1,4,128]{4,3,2,1,0:T(4,128)(2,1)S(1)}, u32[]{:S(2)}, u32[]{:S(2)}) %all-to-all-start.3) | async-done | bytes 1048608 | tf_op jit(solution)/shard_map/all_to_all | solution.py:23
  164.7 28.4 %gather_fusion = bf16[4096,4,128]{2,1,0:T(4,128)(2,1)} fusion(bf16[128,4,128]{2,1,0:T(4,128)(2,1)S(1)} %copy.58, s32[4096]{0:T(1024)S(1)} %broadcast_clamp_fusion), kind=kCustom, calls=%fused_computation | custom fusion | bytes 8404992 | tf_op jit(solution)/shard_map/gather | solution.py:109
  198.6 9.4 %all-to-all-start.4 = ((bf16[128,32,4,128]{3,1,2,0:T(8,128)(2,1)}), bf16[128,32,4,128]{3,1,2,0:T(8,128)(2,1)}, u32[]{:S(2)}, u32[]{:S(2)}) async-start(bf16[128,32,4,128]{3,1,2,0:T(8,128)(2,1)} %copy.60), calls=%async_computation.4 | async-start | bytes 8388608 | tf_op jit(solution)/shard_map/all_to_all | solution.py:110
  207.9 52.4 %all-to-all-done.4 = bf16[128,32,4,128]{3,1,2,0:T(8,128)(2,1)} async-done(((bf16[128,32,4,128]{3,1,2,0:T(8,128)(2,1)}), bf16[128,32,4,128]{3,1,2,0:T(8,128)(2,1)}, u32[]{:S(2)}, u32[]{:S(2)}) %all-to-all-start.4) | async-done | bytes 4194336 | tf_op jit(solution)/shard_map/all_to_all | solution.py:110
  293.3 6.7 %all-reduce.1 = (f32[64]{0:T(128)S(1)}, f32[64]{0:T(128)S(1)}) all-reduce(f32[64]{0:T(128)S(1)} %get-tuple-element.8, f32[64]{0:T(128)S(1)} %get-tuple-element.9), channel_id=1, replica_groups=mesh['obs_0'=4,'obs_1'=4,'lvl_0'=4,'lvl_1'=2] {'obs_1'}, use_global_device_ids=true, to_apply=%region_2.3 | all-reduce | flops 128 | bytes 1024 | tf_op jit(solution)/shard_map/psum | solution.py:31
  300.0 6.9 %all-reduce = (f32[64]{0:T(128)S(1)}, f32[64]{0:T(128)S(1)}) all-reduce(f32[64]{0:T(128)S(1)} %get-tuple-element.6, f32[64]{0:T(128)S(1)} %get-tuple-element.7), channel_id=1, replica_groups=mesh['obs_0'=4,'obs_1'=4,'lvl_0'=4,'lvl_1'=2] {'lvl_0'}, use_global_device_ids=true, to_apply=%region_3.4 | all-reduce | flops 128 | bytes 1024 | tf_op jit(solution)/shard_map/psum | solution.py:31
  306.9 8.8 %all-reduce.3 = (f32[64]{0:T(128)S(1)}, f32[64]{0:T(128)S(1)}) all-reduce(f32[64]{0:T(128)S(1)} %get-tuple-element.4, f32[64]{0:T(128)S(1)} %get-tuple-element.5), channel_id=1, replica_groups=mesh['obs_0'=4,'obs_1'=4,'lvl_0'=4,'lvl_1'=2] {'lvl_1'}, use_global_device_ids=true, to_apply=%region_4.5 | all-reduce | flops 128 | bytes 1024 | tf_op jit(solution)/shard_map/psum | solution.py:31
  318.5 6.9 %psum.120 = f32[64]{0:T(128)S(1)} all-reduce(f32[64]{0:T(128)S(1)} %multiply_reduce_fusion.1), channel_id=1, replica_groups=mesh['obs_0'=4,'obs_1'=4,'lvl_0'=4,'lvl_1'=2] {'obs_0'}, use_global_device_ids=true, to_apply=%region_15.16 | all-reduce | flops 64 | bytes 512 | tf_op jit(solution)/shard_map/psum | solution.py:31
  325.5 6.6 %psum.121 = f32[64]{0:T(128)S(1)} all-reduce(f32[64]{0:T(128)S(1)} %psum.120), channel_id=1, replica_groups=mesh['obs_0'=4,'obs_1'=4,'lvl_0'=4,'lvl_1'=2] {'obs_1'}, use_global_device_ids=true, to_apply=%region_16.17 | all-reduce | flops 64 | bytes 512 | tf_op jit(solution)/shard_map/psum | solution.py:31
  332.1 7.2 %psum.122 = f32[64]{0:T(128)S(1)} all-reduce(f32[64]{0:T(128)S(1)} %psum.121), channel_id=1, replica_groups=mesh['obs_0'=4,'obs_1'=4,'lvl_0'=4,'lvl_1'=2] {'lvl_0'}, use_global_device_ids=true, to_apply=%region_17.18 | all-reduce | flops 64 | bytes 512 | tf_op jit(solution)/shard_map/psum | solution.py:31
  339.2 8.7 %psum.123 = f32[64]{0:T(128)S(1)} all-reduce(f32[64]{0:T(128)S(1)} %psum.122), channel_id=1, replica_groups=mesh['obs_0'=4,'obs_1'=4,'lvl_0'=4,'lvl_1'=2] {'lvl_1'}, use_global_device_ids=true, to_apply=%region_18.19 | all-reduce | flops 64 | bytes 512 | tf_op jit(solution)/shard_map/psum | solution.py:31
  361.5 17.6 %scatter_fusion.1 = bf16[16,256,4,128]{3,0,2,1:T(8,128)(2,1)} fusion(bf16[16,256,4,128]{3,0,2,1:T(8,128)(2,1)} %broadcast.85, s32[128]{0:T(128)S(1)} %fusion.68, bf16[128,16,4,128]{3,1,2,0:T(8,128)(2,1)} %fusion.25), kind=kCustom, calls=%fused_computation.6 | custom fusion | bytes 6291968 | tf_op jit(solution)/shard_map/scatter | solution.py:92
  385.3 56.5 %all_to_all.44 = bf16[128,32,4,128]{3,1,2,0:T(8,128)(2,1)S(1)} all-to-all(bf16[128,32,4,128]{3,1,2,0:T(8,128)(2,1)S(1)} %copy.66), channel_id=1, replica_groups=mesh['obs_0'=4,'obs_1'=4,'lvl_0'=4,'lvl_1'=2] {'obs_0','obs_1','lvl_0','..., dimensions={0} | all-to-all | bytes 8388608 | tf_op jit(solution)/shard_map/all_to_all | solution.py:95
  459.6 18.3 %all_to_all.45 = bf16[8,128,1,4,128]{4,3,2,1,0:T(4,128)(2,1)S(1)} all-to-all(bf16[8,128,1,4,128]{4,3,2,1,0:T(4,128)(2,1)S(1)} %broadcast_in_dim.17), channel_id=1, replica_groups=mesh['obs_0'=4,'obs_1'=4,'lvl_0'=4,'lvl_1'=2] {'lvl_0','lvl_1'}, dimensions={0} | all-to-all | bytes 2097152 | tf_op jit(solution)/shard_map/all_to_all | solution.py:23
  480.4 28.4 %gather_fusion.2 = bf16[4096,4,128]{2,1,0:T(4,128)(2,1)} fusion(bf16[128,4,128]{2,1,0:T(4,128)(2,1)S(1)} %copy.72, s32[4096]{0:T(1024)S(1)} %broadcast_clamp_fusion), kind=kCustom, calls=%fused_computation.2 | custom fusion | bytes 8404992 | tf_op jit(solution)/shard_map/gather | solution.py:109
  512.3 57.2 %all_to_all.46 = bf16[128,32,4,128]{3,1,2,0:T(8,128)(2,1)S(1)} all-to-all(bf16[128,32,4,128]{3,1,2,0:T(8,128)(2,1)S(1)} %copy.74), channel_id=1, replica_groups=mesh['obs_0'=4,'obs_1'=4,'lvl_0'=4,'lvl_1'=2] {'obs_0','obs_1','lvl_0','..., dimensions={0} | all-to-all | bytes 8388608 | tf_op jit(solution)/shard_map/all_to_all | solution.py:110
  601.2 6.7 %psum.125 = f32[64]{0:T(128)S(1)} all-reduce(f32[64]{0:T(128)S(1)} %psum.124), channel_id=1, replica_groups=mesh['obs_0'=4,'obs_1'=4,'lvl_0'=4,'lvl_1'=2] {'obs_1'}, use_global_device_ids=true, to_apply=%region_22.23 | all-reduce | flops 64 | bytes 512 | tf_op jit(solution)/shard_map/psum | solution.py:31
  607.9 6.9 %psum.126 = f32[64]{0:T(128)S(1)} all-reduce(f32[64]{0:T(128)S(1)} %psum.125), channel_id=1, replica_groups=mesh['obs_0'=4,'obs_1'=4,'lvl_0'=4,'lvl_1'=2] {'lvl_0'}, use_global_device_ids=true, to_apply=%region_23.24 | all-reduce | flops 64 | bytes 512 | tf_op jit(solution)/shard_map/psum | solution.py:31
  614.8 8.8 %psum.127 = f32[64]{0:T(128)S(1)} all-reduce(f32[64]{0:T(128)S(1)} %psum.126), channel_id=1, replica_groups=mesh['obs_0'=4,'obs_1'=4,'lvl_0'=4,'lvl_1'=2] {'lvl_1'}, use_global_device_ids=true, to_apply=%region_24.25 | all-reduce | flops 64 | bytes 512 | tf_op jit(solution)/shard_map/psum | solution.py:31
  (83 shorter events, 174.3 us)
Async XLA Ops:
  0.6 20.8 %copy-start = (bf16[128,64,128]{2,1,0:T(8,128)(2,1)S(1)}, bf16[128,64,128]{2,1,0:T(8,128)(2,1)}, u32[]{:S(2)}) copy-start(bf16[128,64,128]{2,1,0:T(8,128)(2,1)} %param.9) | copy-start | bytes 6291460
  5.0 49.7 %all-to-all-start = ((s32[128,1,32]{2,1,0:T(1,128)}), s32[128,1,32]{2,1,0:T(1,128)S(1)}, u32[]{:S(2)}, u32[]{:S(2)}) async-start(s32[128,1,32]{2,1,0:T(1,128)} %bitcast.4), calls=%async_computation | async-start | bytes 131072 | tf_op jit(solution)/shard_map/all_to_all | solution.py:62
  54.7 62.8 %copy-start.3 = (bf16[8,1,128]{2,0,1:T(8,128)(2,1)S(1)}, bf16[8,1,128]{2,0,1:T(8,128)(2,1)}, u32[]{:S(2)}) copy-start(bf16[8,1,128]{2,0,1:T(8,128)(2,1)} %param.12) | copy-start | bytes 6148
  54.7 62.8 %all-to-all-start.1 = ((bf16[128,32,4,128]{3,1,2,0:T(8,128)(2,1)}), bf16[128,32,4,128]{3,1,2,0:T(8,128)(2,1)}, u32[]{:S(2)}, u32[]{:S(2)}) async-start(bf16[128,32,4,128]{3,1,2,0:T(8,128)(2,1)} %copy.52), calls=%async_computation.1 | async-start | bytes 8388608 | tf_op jit(solution)/shard_map/all_to_all | solution.py:95
  118.1 23.1 %all-to-all-start.2 = ((bf16[16,8,1,128]{3,1,2,0:T(8,128)(2,1)}), bf16[16,8,1,128]{3,1,2,0:T(8,128)(2,1)S(1)}, u32[]{:S(2)}, u32[]{:S(2)}) async-start(bf16[16,8,1,128]{3,1,2,0:T(8,128)(2,1)} %broadcast_in_dim.15), calls=%async_computation.2 | async-start | bytes 65536 | tf_op jit(solution)/shard_map/all_to_all | solution.py:23
  130.9 6.5 %copy-start.1 = (bf16[1,128,128]{2,1,0:T(8,128)(2,1)S(1)}, bf16[1,128,128]{2,1,0:T(8,128)(2,1)}, u32[]{:S(2)}) copy-start(bf16[1,128,128]{2,1,0:T(8,128)(2,1)} %param.13) | copy-start | bytes 98308
  142.8 19.4 %all-to-all-start.3 = ((bf16[8,128,1,4,128]{4,3,2,1,0:T(4,128)(2,1)}), bf16[8,128,1,4,128]{4,3,2,1,0:T(4,128)(2,1)S(1)}, u32[]{:S(2)}, u32[]{:S(2)}) async-start(bf16[8,128,1,4,128]{4,3,2,1,0:T(4,128)(2,1)} %broadcast_in_dim.16), calls=%async_computation.3 | async-start | bytes 2097152 | tf_op jit(solution)/shard_map/all_to_all | solution.py:23
  198.6 61.8 %all-to-all-start.4 = ((bf16[128,32,4,128]{3,1,2,0:T(8,128)(2,1)}), bf16[128,32,4,128]{3,1,2,0:T(8,128)(2,1)}, u32[]{:S(2)}, u32[]{:S(2)}) async-start(bf16[128,32,4,128]{3,1,2,0:T(8,128)(2,1)} %copy.60), calls=%async_computation.4 | async-start | bytes 8388608 | tf_op jit(solution)/shard_map/all_to_all | solution.py:110
  279.5 4.8 copy-start.2
where the time goes:
time: 639 us; the launch traced here: 630 us
  blocking collectives  219 us (34%)
  local copies, waits for them, and re-layouts  202 us (32%)
  waiting for transfers between devices  118 us (18%)
  starting transfers between devices  39.2 us (6%)
  matrix products  27.4 us (4%)
  other arithmetic  23 us (4%)
    psum x12, blocking collectives, by_axis(): return functools.reduce(lax.psum, axes, shard)  86.8 us
    all_to_all x1, blocking collectives, on_device(): lax.all_to_all(returning, OBS_LVL, split_axis=0, concat_axis=0, tiled=True)  57.2 us
    gather x2, local copies, waits for them, and re-layouts, on_device(): grid_values[col_rows].reshape(devices, lvl_cap, col_width, node_cols)  56.8 us
    all_to_all x1, blocking collectives, on_device(): lax.all_to_all(outgoing, OBS_LVL, split_axis=0, concat_axis=0, tiled=True)  56.5 us
    all_to_all x1, waiting for transfers between devices, on_device(): lax.all_to_all(returning, OBS_LVL, split_axis=0, concat_axis=0, tiled=True)  52.4 us
    all_to_all x1, waiting for transfers between devices, on_device(): lax.all_to_all(outgoing, OBS_LVL, split_axis=0, concat_axis=0, tiled=True)  51.1 us
    scatter x4, local copies, waits for them, and re-layouts, on_device(): outgoing = jnp.zeros((obs_count, lvl_slots, col_width, node_cols), jnp.bf...  45 us
    all_to_all x1, blocking collectives, from_everyone(): return lax.all_to_all(copies, axis, split_axis=0, concat_axis=0, tiled=True)  18.3 us
  transfers between devices with their start and end apart: 5, of which 3 were waited for; matrix products, arithmetic and copies ran while one was open for 9% of the time, Pallas kernels for 0%

commit v1 on v0

v1 whole, which is shorter than its diff:
```python
import jax
import jax.numpy as jnp
from jax import lax
from jax.sharding import Mesh
from jax.sharding import PartitionSpec as P

ITERS = 2
OBS_LVL = ("obs_0", "obs_1", "lvl_0", "lvl_1")
OBS = ("obs_0", "obs_1")
LVL = ("lvl_0", "lvl_1")
CHIPS = ("obs_0", "obs_1", "lvl_0")
CORE = "lvl_1"


def on_device(rhs, tile_weights, tile_owner, tile_row, axis_a, axis_b, coupling, noise):
    chips = lax.axis_size(CHIPS)
    lvl_count = lax.axis_size(LVL)
    tile_count, tile_obs, node_cols = tile_weights.shape
    columns = rhs.shape[0]
    a_rows, lvl_here, grid_first = axis_a.shape
    levels = lvl_count * lvl_here
    per_chip = columns // chips
    owner = tile_owner[:, 0]
    level = (owner % lvl_count) * lvl_here + tile_row % lvl_here
    first_index = owner // lvl_count * a_rows + tile_row // lvl_here
    place = level * grid_first + first_index
    places = lax.all_gather(place, CHIPS).reshape(chips * tile_count)
    kernel_a = lax.all_gather(axis_a, OBS, axis=0, tiled=True)
    kernel_a = lax.all_gather(kernel_a, LVL, axis=1, tiled=True)
    kernel_b = lax.all_gather(axis_b, LVL, axis=0, tiled=True)
    rows = jnp.arange(levels * grid_first, dtype=jnp.int32)
    collect = (rows[:, None] == places[None, :]).astype(jnp.bfloat16)
    pick = (places[:, None] == rows[None, :]).astype(jnp.bfloat16)

    def axis_pass(field):
        first = jnp.einsum(
            "larb,lbc->larc", field, kernel_b, preferred_element_type=jnp.float32
        ).astype(jnp.bfloat16)
        return jnp.einsum(
            "xla,larc->lxrc", kernel_a, first, preferred_element_type=jnp.float32
        ).astype(jnp.bfloat16)

    def operator(direction):
        low = direction.astype(jnp.bfloat16).reshape(columns, tile_count, tile_obs)
        part = jnp.einsum(
            "ctk,tkn->ctn", low, tile_weights, preferred_element_type=jnp.float32
        ).astype(jnp.bfloat16)
        part = part.reshape(chips, per_chip, tile_count, node_cols)
        part = lax.all_to_all(part, CHIPS, split_axis=0, concat_axis=0, tiled=True)
        part = jnp.swapaxes(part, 1, 2).reshape(chips * tile_count, per_chip * node_cols)
        summed = jnp.dot(collect, part, preferred_element_type=jnp.float32)
        summed = lax.psum(summed, CORE).astype(jnp.bfloat16)
        spread = axis_pass(summed.reshape(levels, grid_first, per_chip, node_cols))
        mixed = jnp.einsum(
            "lm,marc->larc",
            coupling,
            spread.astype(jnp.float32),
            precision=lax.Precision.HIGHEST,
        ).astype(jnp.bfloat16)
        values = axis_pass(mixed).reshape(levels * grid_first, per_chip * node_cols)
        back = jnp.dot(pick, values, preferred_element_type=jnp.float32).astype(jnp.bfloat16)
        back = back.reshape(chips, tile_count, per_chip, node_cols)
        back = jnp.swapaxes(back, 1, 2)
        back = lax.all_to_all(back, CHIPS, split_axis=0, concat_axis=0, tiled=True)
        back = back.reshape(columns, tile_count, node_cols)
        back = jnp.einsum(
            "ctn,tkn->ctk", back, tile_weights, preferred_element_type=jnp.float32
        ).astype(jnp.bfloat16)
        back = back.reshape(columns, tile_count * tile_obs)
        return back.astype(jnp.float32) + noise[:, None] * direction

    def total(field):
        return lax.psum(jnp.sum(field, axis=1), OBS_LVL)

    solution = jnp.zeros_like(rhs)
    residual = rhs
    direction = rhs
    norm_now = total(residual * residual)
    for step in range(ITERS):
        image = operator(direction)
        alpha = norm_now / total(direction * image)
        solution = solution + alpha[:, None] * direction
        residual = residual - alpha[:, None] * image
        if step + 1 < ITERS:
            norm_next = total(residual * residual)
            direction = residual + (norm_next / norm_now)[:, None] * direction
            norm_now = norm_next
    return (solution, residual)


def solution(mesh):
    split = Mesh(mesh.devices.reshape(4, 4, 4, 2), OBS_LVL)
    in_specs = (
        P(None, OBS_LVL),
        P(OBS_LVL, None, None),
        P(OBS_LVL, None),
        P(OBS_LVL),
        P(OBS, LVL, None),
        P(LVL, None, None),
        P(),
        P(),
    )
    out_specs = (P(None, OBS_LVL), P(None, OBS_LVL))
    return jax.shard_map(
        on_device, mesh=split, in_specs=in_specs, out_specs=out_specs, check_vma=False
    )
```

time: 639 us -> 655 us (1.025)
  blocking collectives: 219 us -> 547 us
  local copies, waits for them, and re-layouts: 202 us -> 30.2 us
  waiting for transfers between devices: 118 us -> 0.01 us
  starting transfers between devices: 39.2 us -> 12.4 us
  matrix products: 27.4 us -> 38.1 us
    all_gather x0 -> x4, blocking collectives: none -> 242 us  [the longest x1 147 us: on_device(): places = lax.all_gather(place, CHIPS).reshape(chips * tile_count)]
    all_to_all x5 -> x1, waiting for transfers between devices: 118 us -> 0.01 us  [operator(): part = lax.all_to_all(part, CHIPS, split_axis=0, concat_axis=0, tiled=True)]
    psum x12 -> x5, blocking collectives: 86.8 us -> 201 us  [the longest x3 190 us: total(): return lax.psum(jnp.sum(field, axis=1), OBS_LVL)]
    gather x4 -> x0, local copies, waits for them, and re-layouts: 65.5 us -> none  [the longest x2 56.8 us: on_device(): grid_values[col_rows].reshape(devices, lvl_cap, col_width, node_cols)]
    scatter x5 -> x0, local copies, waits for them, and re-layouts: 46 us -> none  [the longest x4 45 us: on_device(): outgoing = jnp.zeros((obs_count, lvl_slots, col_width, node_cols), jnp.bf...]
    all_to_all x3, blocking collectives: 132 us -> 103 us  [the longest x2 68.6 us: operator(): back = lax.all_to_all(back, CHIPS, split_axis=0, concat_axis=0, tiled=True)]
    all_to_all x5 -> x1, starting transfers between devices: 39.2 us -> 12.4 us  [operator(): part = lax.all_to_all(part, CHIPS, split_axis=0, concat_axis=0, tiled=True)]
    reshape x11 -> x4, local copies, waits for them, and re-layouts: 29.6 us -> 11.5 us  [the longest x2 7.49 us: operator(): low = direction.astype(jnp.bfloat16).reshape(columns, tile_count, tile_obs)]
  transfers between devices with their start and end apart: 5 -> 1, of which waited for: 3 -> 0; matrix products, arithmetic and copies ran while one was open for 9% -> 0% of each run, Pallas kernels for 0% -> 0%
where the time goes in v1:
time: 655 us; the launch traced here: 649 us
  blocking collectives  547 us (84%)
  matrix products  38.1 us (6%)
  local copies, waits for them, and re-layouts  30.2 us (5%)
  other arithmetic  20.7 us (3%)
  starting transfers between devices  12.4 us (2%)
    psum x3, blocking collectives, total(): return lax.psum(jnp.sum(field, axis=1), OBS_LVL)  190 us
    all_gather x1, blocking collectives, on_device(): places = lax.all_gather(place, CHIPS).reshape(chips * tile_count)  147 us
    all_to_all x2, blocking collectives, operator(): back = lax.all_to_all(back, CHIPS, split_axis=0, concat_axis=0, tiled=True)  68.6 us
    all_gather x1, blocking collectives, on_device(): kernel_a = lax.all_gather(kernel_a, LVL, axis=1, tiled=True)  46 us
    all_gather x1, blocking collectives, on_device(): kernel_a = lax.all_gather(axis_a, OBS, axis=0, tiled=True)  36.1 us
    all_to_all x1, blocking collectives, operator(): part = lax.all_to_all(part, CHIPS, split_axis=0, concat_axis=0, tiled=True)  34.4 us
    convert_element_type x4, local copies, waits for them, and re-layouts, operator(): return back.astype(jnp.float32) + noise[:, None] * direction  18.3 us
    dot_general x2, matrix products, operator(): jnp.dot(pick, values, preferred_element_type=jnp.float32)  13.4 us
  transfers between devices with their start and end apart: 1, of which 0 were waited for; matrix products, arithmetic and copies ran while one was open for 0% of the time, Pallas kernels for 0%

profile of v1, /device:TPU:1, one launch (start us, length us, event | category | flops | bytes accessed | tf_op | source)
XLA Modules:
  0.0 649.1 jit_solution(12600232732203647651)
XLA Ops:
  11.7 12.4 %all-to-all-start = ((bf16[64,1,128,128]{3,2,1,0:T(8,128)(2,1)}), bf16[64,1,128,128]{3,2,1,0:T(8,128)(2,1)}, u32[]{:S(2)}, u32[]{:S(2)}) async-start(bf16[64,1,128,128]{3,2,1,0:T(8,128)(2,1)} %copy.23), calls=%async_computation | async-start | bytes 4194304 | tf_op jit(solution)/shard_map/all_to_all | solution.py:49
  24.1 36.1 %all_gather.18 = bf16[128,1,128]{2,0,1:T(8,128)(2,1)S(1)} all-gather(bf16[8,1,128]{2,0,1:T(8,128)(2,1)S(1)} %copy-done.4), channel_id=1, replica_groups=mesh['obs_0'=4,'obs_1'=4,'lvl_0'=4,'lvl_1'=2] {'obs_0','obs_1'}, dimensions={0}, use_global_device_ids=true | all-gather | bytes 34816 | tf_op jit(solution)/shard_map/all_gather | solution.py:28
  60.2 147.0 %all-gather.1 = s32[64,1,128]{2,1,0:T(1,128)S(1)} all-gather(s32[1,1,128]{2,1,0:T(1,128)S(1)} %fusion.40), channel_id=2, replica_groups=mesh['obs_0'=4,'obs_1'=4,'lvl_0'=4,'lvl_1'=2] {'obs_0','obs_1','lvl_0'}, dimensions={0}, use_global_device_ids=true | all-gather | bytes 33280 | tf_op jit(solution)/shard_map/all_gather | solution.py:27
  207.2 46.0 %all_gather.19 = bf16[128,8,128]{2,0,1:T(8,128)(2,1)S(1)} all-gather(bf16[128,1,128]{2,0,1:T(8,128)(2,1)S(1)} %all_gather.18), channel_id=1, replica_groups=mesh['obs_0'=4,'obs_1'=4,'lvl_0'=4,'lvl_1'=2] {'lvl_0','lvl_1'}, dimensions={1}, use_global_device_ids=true | all-gather | bytes 294912 | tf_op jit(solution)/shard_map/all_gather | solution.py:29
  253.2 13.0 %all_gather.17 = bf16[8,128,128]{2,1,0:T(8,128)(2,1)S(1)} all-gather(bf16[1,128,128]{2,1,0:T(8,128)(2,1)S(1)} %copy-done.1), channel_id=1, replica_groups=mesh['obs_0'=4,'obs_1'=4,'lvl_0'=4,'lvl_1'=2] {'lvl_0','lvl_1'}, dimensions={0}, use_global_device_ids=true | all-gather | bytes 294912 | tf_op jit(solution)/shard_map/all_gather | solution.py:30
  266.3 6.9 %fusion.1 = f32[1024,128]{1,0:T(8,128)S(1)} fusion(bf16[8192,128]{1,0:T(8,128)(2,1)} %bitcast.5, s32[8192]{0:T(1024)S(1)} %bitcast.96), kind=kOutput, calls=%fused_computation.2 | convolution fusion | flops 2155872256 | bytes 2654208 | tf_op jit(solution)/shard_map/dot_general | solution.py:51
  273.2 4.8 all-reduce.3
  279.5 6.7 %fusion.8 = bf16[8192,128]{1,0:T(8,128)(2,1)S(1)} fusion(bf16[1024,128]{1,0:T(8,128)(2,1)S(1)} %bitcast.95, s32[8192]{0:T(1024)S(1)} %bitcast.97), kind=kOutput, calls=%fused_computation.10 | convolution fusion | flops 2156920832 | bytes 2392064 | tf_op jit(solution)/shard_map/dot_general | solution.py:61
  286.2 33.6 %all_to_all.20 = bf16[64,1,128,128]{3,2,1,0:T(8,128)(2,1)S(1)} all-to-all(bf16[64,1,128,128]{3,2,1,0:T(8,128)(2,1)S(1)} %bitcast.90), channel_id=1, replica_groups=mesh['obs_0'=4,'obs_1'=4,'lvl_0'=4,'lvl_1'=2] {'obs_0','obs_1','lvl_0'}, dimensions={0} | all-to-all | bytes 4194304 | tf_op jit(solution)/shard_map/all_to_all | solution.py:64
  321.5 4.4 copy.29
  325.9 4.8 reshape.98
  333.4 63.3 %all-reduce = (f32[64]{0:T(128)S(1)}, f32[64]{0:T(128)S(1)}) all-reduce(f32[64]{0:T(128)S(1)} %get-tuple-element.3, f32[64]{0:T(128)S(1)} %get-tuple-element.2), channel_id=1, replica_groups=mesh['obs_0'=4,'obs_1'=4,'lvl_0'=4,'lvl_1'=2] {'obs_0','obs_1','lvl_0','..., use_global_device_ids=true, to_apply=%region_1.2 | all-reduce | flops 128 | bytes 1024 | tf_op jit(solution)/shard_map/psum | solution.py:73
  399.5 63.0 %psum.45 = f32[64]{0:T(128)S(1)} all-reduce(f32[64]{0:T(128)S(1)} %multiply_reduce_fusion.1), channel_id=1, replica_groups=mesh['obs_0'=4,'obs_1'=4,'lvl_0'=4,'lvl_1'=2] {'obs_0','obs_1','lvl_0','..., use_global_device_ids=true, to_apply=%region_6.7 | all-reduce | flops 64 | bytes 512 | tf_op jit(solution)/shard_map/psum | solution.py:73
  462.5 3.7 fusion.41
  466.3 4.2 reshape.93
  475.1 34.4 %all_to_all.21 = bf16[64,1,128,128]{3,2,1,0:T(8,128)(2,1)S(1)} all-to-all(bf16[64,1,128,128]{3,2,1,0:T(8,128)(2,1)S(1)} %copy.31), channel_id=1, replica_groups=mesh['obs_0'=4,'obs_1'=4,'lvl_0'=4,'lvl_1'=2] {'obs_0','obs_1','lvl_0'}, dimensions={0} | all-to-all | bytes 4194304 | tf_op jit(solution)/shard_map/all_to_all | solution.py:49
  509.6 5.3 fusion
  514.9 7.1 %all-reduce.4 = bf16[1024,128]{1,0:T(8,128)(2,1)S(1)} all-reduce(f32[1024,128]{1,0:T(8,128)S(1)} %fusion), channel_id=1, replica_groups=mesh['obs_0'=4,'obs_1'=4,'lvl_0'=4,'lvl_1'=2] {'lvl_1'}, use_global_device_ids=true, to_apply=%region_7.8 | all-reduce | flops 131072 | bytes 786432 | tf_op jit(solution)/shard_map/psum | solution.py:52
  523.4 6.7 %fusion.9 = bf16[8192,128]{1,0:T(8,128)(2,1)S(1)} fusion(bf16[1024,128]{1,0:T(8,128)(2,1)S(1)} %bitcast.94, s32[8192]{0:T(1024)S(1)} %bitcast.99), kind=kOutput, calls=%fused_computation.11 | convolution fusion | flops 2156920832 | bytes 2392064 | tf_op jit(solution)/shard_map/dot_general | solution.py:61
  530.1 35.0 %all_to_all.22 = bf16[64,1,128,128]{3,2,1,0:T(8,128)(2,1)S(1)} all-to-all(bf16[64,1,128,128]{3,2,1,0:T(8,128)(2,1)S(1)} %bitcast.89), channel_id=1, replica_groups=mesh['obs_0'=4,'obs_1'=4,'lvl_0'=4,'lvl_1'=2] {'obs_0','obs_1','lvl_0'}, dimensions={0} | all-to-all | bytes 4194304 | tf_op jit(solution)/shard_map/all_to_all | solution.py:64
  566.9 4.4 copy.37
  571.3 4.8 reshape.99
  579.7 63.3 %psum.47 = f32[64]{0:T(128)S(1)} all-reduce(f32[64]{0:T(128)S(1)} %multiply_reduce_fusion), channel_id=1, replica_groups=mesh['obs_0'=4,'obs_1'=4,'lvl_0'=4,'lvl_1'=2] {'obs_0','obs_1','lvl_0','..., use_global_device_ids=true, to_apply=%region_9.10 | all-reduce | flops 64 | bytes 512 | tf_op jit(solution)/shard_map/psum | solution.py:73
  643.0 5.8 multiply_subtract_fusion
  (38 shorter events, 31.4 us)
Async XLA Ops:
  0.6 5.1 copy-start
  11.7 12.4 %copy-start.4 = (bf16[8,1,128]{2,0,1:T(8,128)(2,1)S(1)}, bf16[8,1,128]{2,0,1:T(8,128)(2,1)}, u32[]{:S(2)}) copy-start(bf16[8,1,128]{2,0,1:T(8,128)(2,1)} %param.12) | copy-start | bytes 6148
  11.7 48.5 %copy-start.5 = (s32[128]{0:T(128)S(1)}, s32[128]{0:T(128)}, u32[]{:S(2)}) copy-start(s32[128]{0:T(128)} %param.11) | copy-start | bytes 1540
  11.7 48.5 %copy-start.6 = (s32[128,1]{0,1:T(1,128)S(1)}, s32[128,1]{0,1:T(1,128)}, u32[]{:S(2)}) copy-start(s32[128,1]{0,1:T(1,128)} %param.10) | copy-start | bytes 1540
  11.7 241.5 %copy-start.1 = (bf16[1,128,128]{2,1,0:T(8,128)(2,1)S(1)}, bf16[1,128,128]{2,1,0:T(8,128)(2,1)}, u32[]{:S(2)}) copy-start(bf16[1,128,128]{2,1,0:T(8,128)(2,1)} %param.13) | copy-start | bytes 98308
  11.7 254.6 %all-to-all-start = ((bf16[64,1,128,128]{3,2,1,0:T(8,128)(2,1)}), bf16[64,1,128,128]{3,2,1,0:T(8,128)(2,1)}, u32[]{:S(2)}, u32[]{:S(2)}) async-start(bf16[64,1,128,128]{3,2,1,0:T(8,128)(2,1)} %copy.23), calls=%async_computation | async-start | bytes 4194304 | tf_op jit(solution)/shard_map/all_to_all | solution.py:49
  273.2 5.5 copy-start.2
  325.9 4.8 copy-start.3

commit v2 on v1

v2 whole, which is shorter than its diff:
```python
import functools

import jax
import jax.numpy as jnp
from jax import lax
from jax.experimental import pallas as pl
from jax.experimental.pallas import tpu as pltpu
from jax.sharding import Mesh
from jax.sharding import PartitionSpec as P

AXES = ("obs_0", "obs_1", "lvl_0", "lvl_1")
OBS = ("obs_0", "obs_1")
LVL = ("lvl_0", "lvl_1")
MESH = pl.DeviceIdType.MESH

SIDE = 4
CHIPS = SIDE**3
LEVELS = 8
GRID_A = 128
NODES = 128
TILES = 128
TILE_OBS = 64
GROUP = 4
GROUPS = CHIPS // GROUP
QUAD = 4
WIDTH = QUAD * TILE_OBS
PITCH = TILES + 8
F32 = jnp.float32
BF16 = jnp.bfloat16


def dot(a, b):
    return jnp.dot(a, b, preferred_element_type=F32)


def two(v):
    return jnp.concatenate([v, v], axis=1)


def kernel(
    rhs_hbm,
    weights_hbm,
    place_ref,
    axis_a_ref,
    axis_b_ref,
    coupling_ref,
    noise_ref,
    noise_rows_ref,
    solution_ref,
    residual_ref,
    rhs_ref,
    weights_ref,
    turn,
    out_buf,
    in_buf,
    ret_buf,
    got_buf,
    places,
    spread_places,
    all_a,
    all_b,
    mat_a,
    acc,
    first_sums,
    partner_acc,
    grid_values,
    passed,
    stat_out,
    stat_in,
    stat_sum,
    stat_partner,
    coef_out,
    coef_in,
    coef_rows,
    load_sem,
    out_sem,
    in_sem,
    ret_sem,
    got_sem,
    place_sem,
    a_sem,
    b_sem,
    ab_sem,
    small_send_sem,
    stat_sem,
    coef_sem,
    acc_send_sem,
    acc_sem,
    tot_send_sem,
    tot_sem,
):
    z, y, x, core = (lax.axis_index(a) for a in AXES)
    me = (z * SIDE + y) * SIDE + x

    def offset(k):
        low, mid, high = k % SIDE, (k // SIDE) % SIDE, k // (SIDE * SIDE)
        return high + mid + low, mid + 2 * low, low

    def ahead(k):
        dz, dy, dx = offset(k)
        return (z + dz) % SIDE, (y + dy) % SIDE, (x + dx) % SIDE

    def behind(k):
        dz, dy, dx = offset(k)
        return (z + 12 - dz) % SIDE, (y + 12 - dy) % SIDE, (x + 12 - dx) % SIDE

    def chip(place):
        return (place[0] * SIDE + place[1]) * SIDE + place[2]

    def remote(src, dst, send, recv, place):
        return pltpu.make_async_remote_copy(
            src, dst, send, recv, device_id=(*place, core), device_id_type=MESH
        )

    def to_partner(src, dst, send, recv):
        return pltpu.make_async_remote_copy(
            src, dst, send, recv, device_id=(z, y, x, 1 - core), device_id_type=MESH
        )

    def local(src, dst, sem):
        pltpu.make_async_copy(src, dst, sem).start()

    def done(ref, sem):
        pltpu.make_async_copy(ref, ref, sem).wait()

    def each(start, stop, body):
        def step(k, unused):
            body(k)
            return unused

        lax.fori_loop(start, stop, step, 0)

    loads = [
        pltpu.make_async_copy(rhs_hbm, rhs_ref, load_sem.at[0]),
        pltpu.make_async_copy(weights_hbm, weights_ref, load_sem.at[1]),
    ]
    for load in loads:
        load.start()
    barrier = pltpu.get_barrier_semaphore()

    @functools.partial(each, 1, CHIPS)
    def _(k):
        pl.semaphore_signal(
            barrier, inc=1, device_id=(*ahead(k), core), device_id_type=MESH
        )

    pl.semaphore_signal(
        barrier, inc=1, device_id=(z, y, x, 1 - core), device_id_type=MESH
    )
    for load in loads:
        load.wait()

    lane = lax.broadcasted_iota(jnp.int32, (CHIPS, WIDTH), 1)
    in_tile = [lane // TILE_OBS == q for q in range(QUAD)]
    half = lax.broadcasted_iota(jnp.int32, (CHIPS, NODES), 1) < TILE_OBS
    rows = lax.broadcasted_iota(jnp.int32, (LEVELS * GRID_A, TILES), 0).astype(F32)
    cols = lax.broadcasted_iota(jnp.int32, (GROUP * TILES, NODES), 1).astype(F32)
    rest = pl.ds(1, CHIPS - 1)

    def window(i):
        return pl.ds(pl.multiple_of(i * WIDTH, WIDTH), WIDTH)

    def column(c):
        return pl.ds(pl.multiple_of(c * PITCH, 8), TILES)

    def spread_out(i, values):
        low = jnp.concatenate(
            [jnp.where(m, values, 0.0).astype(BF16) for m in in_tile], axis=0
        )
        part = dot(low, weights_ref[window(i), :])
        for q in range(QUAD):
            turn[pl.ds(QUAD * i + q, CHIPS, stride=PITCH), :] = part[
                q * CHIPS : (q + 1) * CHIPS
            ]

    def gather_back(i):
        values = jnp.concatenate(
            [
                turn[pl.ds(QUAD * i + q, CHIPS, stride=PITCH), :].astype(BF16)
                for q in range(QUAD)
            ],
            axis=0,
        )
        full = lax.dot_general(
            values,
            weights_ref[window(i), :],
            (((1,), (1,)), ((), ())),
            preferred_element_type=F32,
        )
        parts = []
        for h in range(QUAD // 2):
            lanes = slice(h * NODES, (h + 1) * NODES)
            even = full[2 * h * CHIPS : (2 * h + 1) * CHIPS, lanes]
            odd = full[(2 * h + 1) * CHIPS : (2 * h + 2) * CHIPS, lanes]
            parts.append(jnp.where(half, even, odd))
        return jnp.concatenate(parts, axis=1)

    def folded(product):
        return product[:, :NODES] + product[:, NODES:]

    def stat_rows(index, sums):
        for c in range(CHIPS):
            stat_out[index, c, :, :] = sums[c : c + 1, :]

    def send_parts(stats):
        def pack(k):
            out_buf[k] = turn[column(chip(ahead(k))), :].astype(BF16)

        def copy(k):
            return remote(
                out_buf.at[k], in_buf.at[k], out_sem, in_sem.at[k // GROUP], ahead(k)
            )

        pack(0)
        pack(1)
        local(out_buf.at[0], in_buf.at[0], in_sem.at[0])

        @functools.partial(each, 2, CHIPS)
        def _(k):
            pack(k)
            copy(k - 1).start()

        copy(CHIPS - 1).start()
        for s in range(stats):
            local(stat_out.at[s, me], stat_in.at[s, 0], stat_sem.at[s])

            @functools.partial(each, 1, CHIPS)
            def _(k):
                remote(
                    stat_out.at[s, chip(ahead(k))],
                    stat_in.at[s, k],
                    small_send_sem.at[s],
                    stat_sem.at[s],
                    ahead(k),
                ).start()

    def collect_parts():
        acc[...] = jnp.zeros_like(acc)

        @functools.partial(each, 0, GROUPS)
        def _(g):
            slots = pl.ds(g * GROUP, GROUP)
            done(in_buf.at[slots], in_sem.at[g])
            chosen = jnp.concatenate(
                [
                    jnp.where(rows == places[g * GROUP + j], 1.0, 0.0).astype(BF16)
                    for j in range(GROUP)
                ],
                axis=1,
            )
            parts = in_buf[slots].reshape(GROUP * TILES, NODES)
            acc[...] += dot(chosen, parts).reshape(LEVELS, GRID_A, NODES)

    def exchange(step, stats):
        for s in range(stats):
            done(stat_in.at[s], stat_sem.at[s])
            stat_sum[step, s] = jnp.sum(stat_in[s], axis=0)
        copies = [
            to_partner(
                acc.at[l],
                partner_acc.at[step, l],
                acc_send_sem.at[step, l],
                acc_sem.at[step, l],
            )
            for l in range(LEVELS)
        ]
        for copy in copies:
            copy.start()
        total = to_partner(
            stat_sum.at[step], stat_partner.at[step], tot_send_sem.at[step], tot_sem.at[step]
        )
        total.start()
        return copies, total

    def axis_pass(l, field):
        first = dot(field.astype(BF16), all_b[l % 2, l // 2]).astype(BF16)
        return dot(mat_a[l], first)

    def grid_step(step, copies, beta):
        for l in range(LEVELS):
            copies[l].wait()
            sums = acc[l] + partner_acc[step, l]
            if step:
                sums = sums + beta * first_sums[l]
            first_sums[l] = sums
            passed[l] = axis_pass(l, sums).astype(BF16)
        product = jnp.zeros((8, NODES), F32)
        for l in range(LEVELS):
            mixed = jnp.zeros((GRID_A, NODES), F32)
            for m in range(LEVELS):
                mixed = mixed + coupling_ref[l, m] * passed[m].astype(F32)
            values = axis_pass(l, mixed).astype(BF16)
            grid_values[l * GRID_A : (l + 1) * GRID_A, :] = values
            terms = first_sums[l] * values.astype(F32)
            product = product + jnp.sum(terms.reshape(GRID_A // 8, 8, NODES), axis=0)
        return jnp.sum(product)

    def send_back():
        def copy(k):
            return remote(
                ret_buf.at[k], got_buf.at[me], ret_sem, got_sem.at[k // GROUP], behind(k)
            )

        def pick(g):
            slots = pl.ds(g * GROUP, GROUP)
            where = spread_places[slots].reshape(GROUP * TILES, NODES)
            chosen = jnp.concatenate(
                [
                    jnp.where(where == cols + float(l * NODES), 1.0, 0.0).astype(BF16)
                    for l in range(LEVELS)
                ],
                axis=1,
            )
            ret_buf[slots] = (
                dot(chosen, grid_values[...]).astype(BF16).reshape(GROUP, TILES, NODES)
            )

        pick(0)
        pick(1)
        local(ret_buf.at[0], got_buf.at[me], got_sem.at[0])
        for k in range(1, GROUP):
            copy(k).start()

        @functools.partial(each, 2, GROUPS)
        def _(g):
            pick(g)
            for j in range(GROUP):
                copy((g - 1) * GROUP + j).start()

        for j in range(GROUP):
            copy((GROUPS - 1) * GROUP + j).start()

    def send_coefs(slot):
        local(coef_out.at[slot], coef_in.at[slot, me], coef_sem.at[slot])

        @functools.partial(each, 1, CHIPS)
        def _(k):
            remote(
                coef_out.at[slot],
                coef_in.at[slot, me],
                small_send_sem.at[2 + slot],
                coef_sem.at[slot],
                behind(k),
            ).start()

    def receive_coefs(slot):
        done(coef_in.at[slot], coef_sem.at[slot])
        for c in range(CHIPS):
            coef_rows[slot, c : c + 1, :] = coef_in[slot, c]

    def receive_back():
        @functools.partial(each, 0, GROUPS)
        def _(g):
            done(got_buf.at[pl.ds(g * GROUP, GROUP)], got_sem.at[g])
            for j in range(GROUP):
                c = chip(ahead(g * GROUP + j))
                turn[column(c), :] = got_buf[c].astype(F32)

    def rhs_quad(i, total):
        values = rhs_ref[:, window(i)]
        spread_out(i, values)
        return total + folded(values * values)

    zero = jnp.zeros((CHIPS, NODES), F32)
    total = lax.fori_loop(0, TILES // QUAD, rhs_quad, zero)
    stat_rows(0, total)

    pl.semaphore_wait(barrier, CHIPS)
    own_obs = z * SIDE + y
    local(place_ref, places.at[0], place_sem)
    local(axis_a_ref, all_a.at[core, x, own_obs], a_sem)
    local(axis_b_ref, all_b.at[core, x], b_sem)

    @functools.partial(each, 1, CHIPS)
    def _(k):
        to = ahead(k)
        remote(place_ref, places.at[k], small_send_sem.at[5], place_sem, to).start()
        remote(
            axis_a_ref, all_a.at[core, x, own_obs], small_send_sem.at[6], a_sem, to
        ).start()

    for d in range(1, SIDE):
        remote(
            axis_b_ref,
            all_b.at[core, x],
            small_send_sem.at[7],
            b_sem,
            (z, y, (x + d) % SIDE),
        ).start()
    send_parts(1)

    done(places, place_sem)

    @functools.partial(each, 0, CHIPS)
    def _(k):
        spread_places[k] = jnp.transpose(jnp.broadcast_to(places[k], (TILES, NODES)))

    done(all_a.at[core], a_sem)
    done(all_b.at[core], b_sem)
    shared = [
        to_partner(all_a.at[core], all_a.at[core], small_send_sem.at[8], ab_sem.at[0]),
        to_partner(all_b.at[core], all_b.at[core], small_send_sem.at[9], ab_sem.at[1]),
    ]
    for copy in shared:
        copy.start()
    for copy in shared:
        copy.wait()
    for l in range(LEVELS):
        mat_a[l] = all_a[l % 2, l // 2].astype(F32).reshape(GRID_A, GRID_A).astype(BF16)

    collect_parts()
    copies, total = exchange(0, 1)
    product = grid_step(0, copies, None)
    send_back()
    total.wait()
    norm_first = jnp.sum(stat_sum[0, 0] + stat_partner[0, 0])
    my_noise = noise_ref[me]
    coef_out[0] = jnp.full((1, NODES), norm_first) / jnp.full(
        (1, NODES), product + my_noise * norm_first
    )
    send_coefs(0)

    receive_back()
    receive_coefs(0)
    done(out_buf.at[rest], out_sem)
    done(stat_out.at[0, rest], small_send_sem.at[0])

    def residual_quad(i, carry):
        total, cross = carry
        start = rhs_ref[:, window(i)]
        image = gather_back(i) + two(noise_rows_ref[...]) * start
        values = start - two(coef_rows[0]) * image
        residual_ref[:, window(i)] = values
        spread_out(i, values)
        return total + folded(values * values), cross + folded(values * start)

    total, cross = lax.fori_loop(0, TILES // QUAD, residual_quad, (zero, zero))
    stat_rows(0, total)
    stat_rows(1, cross)
    send_parts(2)
    collect_parts()
    copies, total = exchange(1, 2)
    total.wait()
    norm_next = jnp.sum(stat_sum[1, 0] + stat_partner[1, 0])
    crossed = jnp.sum(stat_sum[1, 1] + stat_partner[1, 1])
    beta = jnp.full((1, NODES), norm_next) / jnp.full((1, NODES), norm_first)
    done(ret_buf.at[rest], ret_sem)
    coef_out[1] = beta
    product = grid_step(1, copies, beta)
    send_back()
    length = norm_next + 2.0 * beta * crossed + beta * beta * norm_first
    coef_out[2] = jnp.full((1, NODES), norm_next) / (product + my_noise * length)
    send_coefs(1)
    send_coefs(2)

    receive_back()
    receive_coefs(1)
    receive_coefs(2)

    def final_quad(i, unused):
        start = rhs_ref[:, window(i)]
        left = residual_ref[:, window(i)]
        direction = left + two(coef_rows[1]) * start
        image = gather_back(i) + two(noise_rows_ref[...]) * direction
        alpha = two(coef_rows[2])
        solution_ref[:, window(i)] = two(coef_rows[0]) * start + alpha * direction
        residual_ref[:, window(i)] = left - alpha * image
        return unused

    lax.fori_loop(0, TILES // QUAD, final_quad, 0)

    done(out_buf.at[rest], out_sem)
    done(ret_buf.at[rest], ret_sem)
    for s in range(2):
        done(stat_out.at[s, rest], small_send_sem.at[s])
    for slot in range(3):
        done(coef_in.at[slot, rest], small_send_sem.at[2 + slot])
    done(places.at[rest], small_send_sem.at[5])
    done(turn.at[pl.ds(0, (CHIPS - 1) * 4)], small_send_sem.at[6])
    done(all_b.at[0, pl.ds(1, SIDE - 1)], small_send_sem.at[7])


def on_device(rhs, tile_weights, tile_owner, tile_row, axis_a, axis_b, coupling, noise):
    lvl_count = lax.axis_size(LVL)
    tile_count, tile_obs, node_cols = tile_weights.shape
    columns, width = rhs.shape
    a_rows, lvl_here, grid_first = axis_a.shape
    owner = tile_owner[:, 0]
    level = (owner % lvl_count) * lvl_here + tile_row % lvl_here
    first_index = owner // lvl_count * a_rows + tile_row // lvl_here
    place = (level * grid_first + first_index).astype(F32).reshape(1, tile_count)
    anywhere = pl.BlockSpec(memory_space=pl.ANY)
    vmem = pl.BlockSpec(memory_space=pltpu.VMEM)
    smem = pl.BlockSpec(memory_space=pltpu.SMEM)
    dma = pltpu.SemaphoreType.DMA
    whole = jax.ShapeDtypeStruct((columns, width), F32)
    slots = (CHIPS, TILES, NODES)
    return pl.pallas_call(
        kernel,
        out_shape=(whole, whole),
        in_specs=[anywhere, anywhere, vmem, vmem, vmem, smem, smem, vmem],
        out_specs=(vmem, vmem),
        scratch_shapes=[
            pltpu.VMEM((columns, width), F32),
            pltpu.VMEM((tile_count * tile_obs, node_cols), BF16),
            pltpu.VMEM((CHIPS * PITCH, NODES), F32),
            pltpu.VMEM(slots, BF16),
            pltpu.VMEM(slots, BF16),
            pltpu.VMEM(slots, BF16),
            pltpu.VMEM(slots, BF16),
            pltpu.VMEM((CHIPS, 1, TILES), F32),
            pltpu.VMEM(slots, F32),
            pltpu.VMEM((2, SIDE, SIDE * SIDE, a_rows, grid_first), BF16),
            pltpu.VMEM((2, SIDE, NODES, NODES), BF16),
            pltpu.VMEM((LEVELS, GRID_A, GRID_A), BF16),
            pltpu.VMEM((LEVELS, GRID_A, NODES), F32),
            pltpu.VMEM((LEVELS, GRID_A, NODES), F32),
            pltpu.VMEM((2, LEVELS, GRID_A, NODES), F32),
            pltpu.VMEM((LEVELS * GRID_A, NODES), BF16),
            pltpu.VMEM((LEVELS, GRID_A, NODES), BF16),
            pltpu.VMEM((2, CHIPS, 1, NODES), F32),
            pltpu.VMEM((2, CHIPS, 1, NODES), F32),
            pltpu.VMEM((2, 2, 1, NODES), F32),
            pltpu.VMEM((2, 2, 1, NODES), F32),
            pltpu.VMEM((3, 1, NODES), F32),
            pltpu.VMEM((3, CHIPS, 1, NODES), F32),
            pltpu.VMEM((3, CHIPS, NODES), F32),
            dma((2,)),
            dma,
            dma((GROUPS,)),
            dma,
            dma((GROUPS,)),
            dma,
            dma,
            dma,
            dma((2,)),
            dma((10,)),
            dma((2,)),
            dma((3,)),
            dma((2, LEVELS)),
            dma((2, LEVELS)),
            dma((2,)),
            dma((2,)),
        ],
        compiler_params=pltpu.CompilerParams(
            collective_id=0, has_side_effects=True, vmem_limit_bytes=60 << 20
        ),
        name="conjugate_gradients",
    )(
        rhs,
        tile_weights.reshape(tile_count * tile_obs, node_cols),
        place,
        axis_a.reshape(a_rows, grid_first),
        axis_b.reshape(node_cols, node_cols),
        coupling,
        noise,
        jnp.broadcast_to(noise[:, None], (columns, NODES)),
    )


def solution(mesh):
    split = Mesh(mesh.devices.reshape(SIDE, SIDE, SIDE, 2), AXES)
    in_specs = (
        P(None, AXES),
        P(AXES, None, None),
        P(AXES, None),
        P(AXES),
        P(OBS, LVL, None),
        P(LVL, None, None),
        P(),
        P(),
    )
    out_specs = (P(None, AXES), P(None, AXES))
    return jax.shard_map(
        on_device, mesh=split, in_specs=in_specs, out_specs=out_specs, check_vma=False
    )
```

time: 655 us -> 168 us (0.26)
  blocking collectives: 547 us -> 0 us
  Pallas kernels: 0 us -> 160 us
  matrix products: 38.1 us -> 0 us
  local copies, waits for them, and re-layouts: 30.2 us -> 5.88 us
  other arithmetic: 20.7 us -> 1.2 us
  starting transfers between devices: 12.4 us -> 0 us
    all_gather x4 -> x0, blocking collectives: 242 us -> none  [the longest x1 147 us: on_device(): places = lax.all_gather(place, CHIPS).reshape(chips * tile_count)]
    psum x5 -> x0, blocking collectives: 201 us -> none  [the longest x3 190 us: total(): return lax.psum(jnp.sum(field, axis=1), OBS_LVL)]
    pallas_call x0 -> x1, Pallas kernels: none -> 160 us  [on_device(): pl.pallas_call(kernel, out_shape=(whole, whole), in_specs=[anywhere, anyw...]
    all_to_all x3 -> x0, blocking collectives: 103 us -> none  [the longest x2 68.6 us: operator(): back = lax.all_to_all(back, CHIPS, split_axis=0, concat_axis=0, tiled=True)]
    dot_general x14 -> x0, matrix products: 38.1 us -> none  [the longest x2 13.4 us: operator(): jnp.dot(pick, values, preferred_element_type=jnp.float32)]
    convert_element_type x6 -> x0, local copies, waits for them, and re-layouts: 18.6 us -> none  [the longest x4 18.3 us: operator(): return back.astype(jnp.float32) + noise[:, None] * direction]
    all_to_all x1 -> x0, starting transfers between devices: 12.4 us -> none  [operator(): part = lax.all_to_all(part, CHIPS, split_axis=0, concat_axis=0, tiled=True)]
    reshape x4 -> x0, local copies, waits for them, and re-layouts: 11.5 us -> none  [the longest x2 7.49 us: operator(): low = direction.astype(jnp.bfloat16).reshape(columns, tile_count, tile_obs)]
  transfers between devices with their start and end apart: 1 -> 0, of which waited for: 0 -> 0; matrix products, arithmetic and copies ran while one was open for 0% -> 0% of each run, Pallas kernels for 0% -> 0%
where the time goes in v2:
time: 168 us
  Pallas kernels  160 us (95%)
  local copies, waits for them, and re-layouts  5.88 us (4%)
    pallas_call x1, Pallas kernels, on_device(): pl.pallas_call(kernel, out_shape=(whole, whole), in_specs=[anywhere, anyw...  160 us
    unnamed x4, local copies, waits for them, and re-layouts  4.53 us

profile of v2, /device:TPU:1, one launch (start us, length us, event | category | flops | bytes accessed | tf_op | source)
XLA Modules:
  0.0 167.8 jit_solution(10354142797290325048)
XLA Ops:
  0.6 1.2 convert_bitcast_fusion.place_ref
  1.8 1.3 broadcast_in_dim.2.noise_rows_ref
  3.2 160.0 %conjugate_gradients.1 = (f32[64,8192]{1,0:T(8,128)}, f32[64,8192]{1,0:T(8,128)}) custom-call(f32[64,8192]{1,0:T(8,128)} %rhs_hbm.1, bf16[8192,128]{1,0:T(8,128)(2,1)} %bitcast.20, f32[1,128]{1,0:T(1,128)} %convert_bitcast_fusion.place_ref, bf16[8,128]{1,0:T(8,128)(2,1)} %bitcast.22, bf16[128,128]{1,0:T(8,128)(2,1)} %bitcast.21, f32[8,8]{1,0:T(8,128)} %coupling_ref.1, ...), custom_call_target="tpu_custom_call" | custom-call | tf_op jit(solution)/shard_map/conjugate_gradients/pallas_call | solution.py:498
  163.2 0.0 copy-start
  163.2 3.2 %copy.12 = f32[64,8192]{1,0:T(8,128)} copy(f32[64,8192]{1,0:T(8,128)} %get-tuple-element.4) | data formatting | bytes 4194304
  166.4 0.0 copy-done
  166.4 1.3 copy.13
Async XLA Ops:
  163.2 3.2 %copy-start = (f32[64,8192]{1,0:T(8,128)S(1)}, f32[64,8192]{1,0:T(8,128)}, u32[]{:S(2)}) copy-start(f32[64,8192]{1,0:T(8,128)} %get-tuple-element.5) | copy-start | bytes 6291460

commit v3 on v2

v3 whole, which is shorter than its diff:
```python
import functools

import jax
import jax.numpy as jnp
from jax import lax
from jax.experimental import pallas as pl
from jax.experimental.pallas import tpu as pltpu
from jax.sharding import Mesh
from jax.sharding import PartitionSpec as P

AXES = ("obs_0", "obs_1", "lvl_0", "lvl_1")
OBS = ("obs_0", "obs_1")
LVL = ("lvl_0", "lvl_1")
MESH = pl.DeviceIdType.MESH

SIDE = 4
CHIPS = SIDE**3
LEVELS = 8
GRID_A = 128
NODES = 128
TILES = 128
TILE_OBS = 64
PARTS = 2
PART = TILES // PARTS
GROUP = 8
GROUPS = CHIPS // GROUP
QUAD = 4
WIDTH = QUAD * TILE_OBS
PAIRS = PART // QUAD // 2
PITCH = TILES + 8
F32 = jnp.float32
BF16 = jnp.bfloat16


def dot(a, b):
    return jnp.dot(a, b, preferred_element_type=F32)


def two(v):
    return jnp.concatenate([v, v], axis=1)


def kernel(
    rhs_hbm,
    weights_hbm,
    owner_ref,
    row_ref,
    axis_a_ref,
    axis_b_ref,
    coupling_ref,
    noise_ref,
    solution_ref,
    residual_ref,
    rhs_ref,
    weights_ref,
    turn,
    out_buf,
    in_buf,
    ret_buf,
    got_buf,
    place_out,
    places,
    part_places,
    spread_places,
    all_a,
    all_b,
    mat_a,
    acc,
    node_sums,
    partner_acc,
    grid_values,
    passed,
    noise_rows,
    stat_out,
    stat_in,
    stat_sum,
    stat_partner,
    coef_out,
    coef_in,
    coef_rows,
    load_sem,
    out_sem,
    in_sem,
    ret_sem,
    got_sem,
    place_sem,
    a_sem,
    b_sem,
    ab_sem,
    small_sem,
    stat_sem,
    coef_sem,
    acc_send_sem,
    acc_sem,
    tot_send_sem,
    tot_sem,
):
    z, y, x, core = (lax.axis_index(a) for a in AXES)
    me = (z * SIDE + y) * SIDE + x
    mine = z * SIDE + y
    x_ahead = [lax.rem(x + d, SIDE) for d in range(SIDE)]
    x_behind = [lax.rem(x + SIDE - d, SIDE) for d in range(SIDE)]

    def ahead(q):
        places = []
        for j in range(GROUP):
            low, mid = j % SIDE, 2 * lax.rem(q, 2) + j // SIDE
            high = lax.div(q, 2)
            places.append(
                (
                    lax.rem(z + high + mid + low, SIDE),
                    lax.rem(y + mid + 2 * low, SIDE),
                    x_ahead[low],
                )
            )
        return places

    def behind(q):
        places = []
        for j in range(GROUP):
            low, mid = j % SIDE, 2 * lax.rem(q, 2) + j // SIDE
            high = lax.div(q, 2)
            places.append(
                (
                    lax.rem(z + 12 - (high + mid + low), SIDE),
                    lax.rem(y + 12 - (mid + 2 * low), SIDE),
                    x_behind[low],
                )
            )
        return places

    def chip(place):
        return (place[0] * SIDE + place[1]) * SIDE + place[2]

    def remote(src, dst, send, recv, place):
        return pltpu.make_async_remote_copy(
            src, dst, send, recv, device_id=(*place, core), device_id_type=MESH
        )

    def to_partner(src, dst, send, recv):
        return pltpu.make_async_remote_copy(
            src, dst, send, recv, device_id=(z, y, x, 1 - core), device_id_type=MESH
        )

    def local(src, dst, sem):
        pltpu.make_async_copy(src, dst, sem).start()

    def done(ref, sem):
        pltpu.make_async_copy(ref, ref, sem).wait()

    def each(start, stop, body):
        def step(k, unused):
            body(k)
            return unused

        lax.fori_loop(start, stop, step, 0)

    def others(places_of, body):
        def group(q, first):
            places = places_of(q)
            for j in range(first, GROUP):
                body(q * GROUP + j, places[j])

        group(0, 1)
        each(1, GROUPS, lambda q: group(q, 0))

    loads = []
    for h in range(PARTS):
        obs = pl.ds(h * PART * TILE_OBS, PART * TILE_OBS)
        loads.append(
            (
                pltpu.make_async_copy(rhs_hbm.at[:, obs], rhs_ref.at[:, obs], load_sem.at[0, h]),
                pltpu.make_async_copy(
                    weights_hbm.at[obs], weights_ref.at[obs], load_sem.at[1, h]
                ),
            )
        )
        for load in loads[h]:
            load.start()
    barrier = pltpu.get_barrier_semaphore()

    def greet(place):
        pl.semaphore_signal(barrier, inc=1, device_id=place, device_id_type=MESH)

    others(ahead, lambda k, place: greet((*place, core)))
    greet((z, y, x, 1 - core))

    lane = lax.broadcasted_iota(jnp.int32, (CHIPS, WIDTH), 1)
    in_tile = [lane // TILE_OBS == q for q in range(QUAD)]
    half = lax.broadcasted_iota(jnp.int32, (CHIPS, NODES), 1) < TILE_OBS
    rows = lax.broadcasted_iota(jnp.int32, (LEVELS * GRID_A, NODES), 0).astype(F32)
    cols = lax.broadcasted_iota(jnp.int32, (GROUP * PART, NODES), 1).astype(F32)
    rest = pl.ds(1, CHIPS - 1)

    owner = owner_ref[...]
    base = (owner & (LEVELS - 1)) * GRID_A + (owner >> 3) * (GRID_A // 16)
    base = jnp.transpose(jnp.broadcast_to(base.astype(F32), (TILES, NODES)))
    place_out[...] = base[0:1, :] + row_ref[...].astype(F32)

    def window(i):
        return pl.ds(pl.multiple_of(i * WIDTH, WIDTH), WIDTH)

    def column(c, h):
        return pl.ds(pl.multiple_of(c * PITCH + h * PART, 8), PART)

    def tile(t):
        return pl.ds(t, CHIPS, stride=PITCH)

    def spread_out(quads, values):
        parts = []
        for i, v in zip(quads, values):
            low = jnp.concatenate(
                [jnp.where(m, v, 0.0).astype(BF16) for m in in_tile], axis=0
            )
            parts.append(dot(low, weights_ref[window(i), :]))
        for i, part in zip(quads, parts):
            for q in range(QUAD):
                turn[tile(QUAD * i + q), :] = part[q * CHIPS : (q + 1) * CHIPS]

    def gather_back(quads):
        fulls = []
        for i in quads:
            values = jnp.concatenate(
                [turn[tile(QUAD * i + q), :].astype(BF16) for q in range(QUAD)], axis=0
            )
            fulls.append(
                lax.dot_general(
                    values,
                    weights_ref[window(i), :],
                    (((1,), (1,)), ((), ())),
                    preferred_element_type=F32,
                )
            )
        out = []
        for full in fulls:
            parts = []
            for p in range(QUAD // 2):
                lanes = slice(p * NODES, (p + 1) * NODES)
                even = full[2 * p * CHIPS : (2 * p + 1) * CHIPS, lanes]
                odd = full[(2 * p + 1) * CHIPS : (2 * p + 2) * CHIPS, lanes]
                parts.append(jnp.where(half, even, odd))
            out.append(jnp.concatenate(parts, axis=1))
        return out

    def folded(product):
        return product[:, :NODES] + product[:, NODES:]

    def send_part(h):
        def pack(q):
            for j, place in enumerate(ahead(q)):
                out_buf[h, q * GROUP + j] = turn[column(chip(place), h), :].astype(BF16)

        def start(q, first=0):
            for j, place in list(enumerate(ahead(q)))[first:]:
                k = q * GROUP + j
                remote(
                    out_buf.at[h, k], in_buf.at[h, k], out_sem.at[h], in_sem.at[h, q], place
                ).start()

        pack(0)
        pack(1)
        local(out_buf.at[h, 0], in_buf.at[h, 0], in_sem.at[h, 0])
        start(0, 1)

        @functools.partial(each, 2, GROUPS)
        def _(q):
            pack(q)
            start(q - 1)

        start(GROUPS - 1)

    def send_stats(first, second):
        for c in range(CHIPS):
            stat_out[c, :, :NODES] = first[c : c + 1, :]
            stat_out[c, :, NODES:] = second[c : c + 1, :]
        local(stat_out.at[me], stat_in.at[0], stat_sem)
        others(
            ahead,
            lambda k, place: remote(
                stat_out.at[chip(place)], stat_in.at[k], small_sem.at[0], stat_sem, place
            ).start(),
        )

    def collect_part(h):
        per_row = NODES // PART
        group_rows = GROUP // per_row

        @functools.partial(each, 0, GROUPS)
        def _(q):
            slots = pl.ds(q * GROUP, GROUP)
            done(in_buf.at[h, slots], in_sem.at[h, q])
            chosen = jnp.concatenate(
                [
                    jnp.where(rows == part_places[h, q * group_rows + j], 1.0, 0.0).astype(BF16)
                    for j in range(group_rows)
                ],
                axis=1,
            )
            parts = in_buf[h, slots].reshape(GROUP * PART, NODES)
            acc[...] += dot(chosen, parts).reshape(LEVELS, GRID_A, NODES)

    def exchange(step):
        copies = [
            to_partner(
                acc.at[l],
                partner_acc.at[step, l],
                acc_send_sem.at[step, l],
                acc_sem.at[step, l],
            )
            for l in range(LEVELS)
        ]
        for copy in copies:
            copy.start()
        done(stat_in, stat_sem)
        stat_sum[step] = jnp.sum(stat_in[...], axis=0)
        total = to_partner(
            stat_sum.at[step], stat_partner.at[step], tot_send_sem.at[step], tot_sem.at[step]
        )
        total.start()
        return copies, total

    def axis_passes(fields):
        firsts = [
            dot(field.astype(BF16), all_b[l % 2, l // 2]).astype(BF16)
            for l, field in enumerate(fields)
        ]
        return [dot(mat_a[l], first).astype(BF16) for l, first in enumerate(firsts)]

    def grid_step(step, copies, beta):
        for copy in copies:
            copy.wait()
        fields = []
        for l in range(LEVELS):
            sums = acc[l] + partner_acc[step, l]
            if step:
                sums = sums + beta * node_sums[l]
            node_sums[l] = sums
            fields.append(sums)
        for l, spread in enumerate(axis_passes(fields)):
            passed[l] = spread
        fields = []
        for l in range(LEVELS):
            mixed = coupling_ref[l, 0] * passed[0].astype(F32)
            for m in range(1, LEVELS):
                mixed = mixed + coupling_ref[l, m] * passed[m].astype(F32)
            fields.append(mixed)
        for l, values in enumerate(axis_passes(fields)):
            grid_values[l * GRID_A : (l + 1) * GRID_A, :] = values

    def curvature():
        product = jnp.zeros((8, NODES), F32)
        for l in range(LEVELS):
            terms = node_sums[l] * grid_values[l * GRID_A : (l + 1) * GRID_A, :].astype(F32)
            product = product + jnp.sum(terms.reshape(GRID_A // 8, 8, NODES), axis=0)
        return jnp.sum(product)

    def send_back(h, between):
        def pick(q):
            slots = pl.ds(q * GROUP, GROUP)
            where = spread_places[slots, pl.ds(h * PART, PART)].reshape(GROUP * PART, NODES)
            chosen = jnp.concatenate(
                [
                    jnp.where(where == cols + float(l * NODES), 1.0, 0.0).astype(BF16)
                    for l in range(LEVELS)
                ],
                axis=1,
            )
            ret_buf[h, slots] = (
                dot(chosen, grid_values[...]).astype(BF16).reshape(GROUP, PART, NODES)
            )

        def start(q, first=0):
            for j, place in list(enumerate(behind(q)))[first:]:
                remote(
                    ret_buf.at[h, q * GROUP + j],
                    got_buf.at[h, me],
                    ret_sem.at[h],
                    got_sem.at[h, q],
                    place,
                ).start()

        pick(0)
        between()
        local(ret_buf.at[h, 0], got_buf.at[h, me], got_sem.at[h, 0])
        start(0, 1)
        pick(1)

        @functools.partial(each, 2, GROUPS)
        def _(q):
            start(q - 1)
            pick(q)

        start(GROUPS - 1)

    def send_coefs(step):
        local(coef_out.at[step], coef_in.at[step, me], coef_sem.at[step])
        others(
            behind,
            lambda k, place: remote(
                coef_out.at[step],
                coef_in.at[step, me],
                small_sem.at[1 + step],
                coef_sem.at[step],
                place,
            ).start(),
        )

    def receive_coefs(step):
        done(coef_in.at[step], coef_sem.at[step])
        for c in range(CHIPS):
            coef_rows[step, c : c + 1, :] = coef_in[step, c]

    def receive_part(h):
        @functools.partial(each, 0, GROUPS)
        def _(q):
            done(got_buf.at[h, pl.ds(q * GROUP, GROUP)], got_sem.at[h, q])
            for place in ahead(q):
                c = chip(place)
                turn[column(c, h), :] = got_buf[h, c].astype(F32)

    def over_part(h, body, carry):
        def step(p, carry):
            i = h * PAIRS * 2 + 2 * p
            return body((i, i + 1), carry)

        return lax.fori_loop(0, PAIRS, step, carry)

    def rhs_quads(quads, total):
        values = [rhs_ref[:, window(i)] for i in quads]
        spread_out(quads, values)
        for v in values:
            total = total + folded(v * v)
        return total

    zero = jnp.zeros((CHIPS, NODES), F32)
    total = zero
    for h in range(PARTS):
        for load in loads[h]:
            load.wait()
        total = over_part(h, rhs_quads, total)
        if h == 0:
            pl.semaphore_wait(barrier, CHIPS)
        send_part(h)
        if h == 0:
            local(place_out, places.at[0], place_sem)
            local(axis_a_ref, all_a.at[core, x, mine], a_sem)
            local(axis_b_ref, all_b.at[core, x], b_sem)

            def introduce(k, place):
                remote(place_out, places.at[k], small_sem.at[3], place_sem, place).start()
                remote(
                    axis_a_ref, all_a.at[core, x, mine], small_sem.at[4], a_sem, place
                ).start()

            others(ahead, introduce)
            for d in range(1, SIDE):
                remote(
                    axis_b_ref, all_b.at[core, x], small_sem.at[5], b_sem, (z, y, x_ahead[d])
                ).start()
    send_stats(total, total)

    for c in range(CHIPS):
        noise_rows[c : c + 1, :] = jnp.full((1, NODES), noise_ref[c])
    acc[...] = jnp.zeros_like(acc)
    done(places, place_sem)

    @functools.partial(each, 0, CHIPS)
    def _(k):
        spread_places[k] = jnp.transpose(jnp.broadcast_to(places[k], (TILES, NODES)))

    first_half = lax.broadcasted_iota(jnp.int32, (1, NODES), 1) < PART

    @functools.partial(each, 0, CHIPS // 2)
    def _(r):
        even, odd = places[2 * r], places[2 * r + 1]
        part_places[0, r] = jnp.where(first_half, even, pltpu.roll(odd, PART, 1))
        part_places[1, r] = jnp.where(first_half, pltpu.roll(even, PART, 1), odd)

    done(all_a.at[core], a_sem)
    done(all_b.at[core], b_sem)
    shared = [
        to_partner(all_a.at[core], all_a.at[core], small_sem.at[6], ab_sem.at[0]),
        to_partner(all_b.at[core], all_b.at[core], small_sem.at[7], ab_sem.at[1]),
    ]
    for copy in shared:
        copy.start()
    collect_part(0)
    for copy in shared:
        copy.wait()
    for l in range(LEVELS):
        mat_a[l] = all_a[l % 2, l // 2].astype(F32).reshape(GRID_A, GRID_A).astype(BF16)
    for h in range(1, PARTS):
        collect_part(h)
    copies, total = exchange(0)
    grid_step(0, copies, None)
    total.wait()
    norm_first = jnp.sum((stat_sum[0] + stat_partner[0])[:, :NODES])
    my_noise = noise_ref[me]

    def first_coefs():
        alpha = jnp.full((1, NODES), norm_first) / jnp.full(
            (1, NODES), curvature() + my_noise * norm_first
        )
        coef_out[0] = two(alpha)

    send_back(0, first_coefs)
    send_coefs(0)
    for h in range(1, PARTS):
        send_back(h, lambda: None)

    def residual_quads(quads, carry):
        total, cross = carry
        backs = gather_back(quads)
        values = []
        for i, back in zip(quads, backs):
            start = rhs_ref[:, window(i)]
            image = back + two(noise_rows[...]) * start
            v = start - coef_rows[0] * image
            residual_ref[:, window(i)] = v
            total = total + folded(v * v)
            cross = cross + folded(v * start)
            values.append(v)
        spread_out(quads, values)
        return total, cross

    acc[...] = jnp.zeros_like(acc)
    carry = (zero, zero)
    for h in range(PARTS):
        receive_part(h)
        if h == 0:
            receive_coefs(0)
        carry = over_part(h, residual_quads, carry)
        done(out_buf.at[h, rest], out_sem.at[h])
        send_part(h)
    done(stat_out.at[rest], small_sem.at[0])
    send_stats(*carry)
    for h in range(PARTS):
        collect_part(h)
    copies, total = exchange(1)
    total.wait()
    stats = stat_sum[1] + stat_partner[1]
    norm_next = jnp.sum(stats[:, :NODES])
    crossed = jnp.sum(stats[:, NODES:])
    beta = jnp.full((1, NODES), norm_next) / jnp.full((1, NODES), norm_first)
    grid_step(1, copies, beta)

    def second_coefs():
        length = norm_next + 2.0 * beta * crossed + beta * beta * norm_first
        alpha = jnp.full((1, NODES), norm_next) / (curvature() + my_noise * length)
        coef_out[1] = jnp.concatenate([alpha, beta], axis=1)

    for h in range(PARTS):
        done(ret_buf.at[h, rest], ret_sem.at[h])
    send_back(0, second_coefs)
    send_coefs(1)
    for h in range(1, PARTS):
        send_back(h, lambda: None)

    def final_quads(quads, carry):
        backs = gather_back(quads)
        alpha, beta = two(coef_rows[1, :, :NODES]), two(coef_rows[1, :, NODES:])
        for i, back in zip(quads, backs):
            start = rhs_ref[:, window(i)]
            left = residual_ref[:, window(i)]
            direction = left + beta * start
            image = back + two(noise_rows[...]) * direction
            solution_ref[:, window(i)] = coef_rows[0] * start + alpha * direction
            residual_ref[:, window(i)] = left - alpha * image
        return carry

    for h in range(PARTS):
        receive_part(h)
        if h == 0:
            receive_coefs(1)
        over_part(h, final_quads, 0)

    for h in range(PARTS):
        done(out_buf.at[h, rest], out_sem.at[h])
        done(ret_buf.at[h, rest], ret_sem.at[h])
    done(stat_out.at[rest], small_sem.at[0])
    for step in range(2):
        done(coef_in.at[step, rest], small_sem.at[1 + step])
    done(places.at[rest], small_sem.at[3])
    done(turn.at[pl.ds(0, (CHIPS - 1) * 4)], small_sem.at[4])
    done(all_b.at[0, pl.ds(1, SIDE - 1)], small_sem.at[5])


def on_device(rhs, tile_weights, tile_owner, tile_row, axis_a, axis_b, coupling, noise):
    tile_count, tile_obs, node_cols = tile_weights.shape
    columns, width = rhs.shape
    a_rows, lvl_here, grid_first = axis_a.shape
    anywhere = pl.BlockSpec(memory_space=pl.ANY)
    vmem = pl.BlockSpec(memory_space=pltpu.VMEM)
    smem = pl.BlockSpec(memory_space=pltpu.SMEM)
    dma = pltpu.SemaphoreType.DMA
    whole = pltpu.VMEM((columns, width), F32)
    parts = pltpu.VMEM((PARTS, CHIPS, PART, NODES), BF16)
    field = pltpu.VMEM((LEVELS, GRID_A, NODES), F32)
    return pl.pallas_call(
        kernel,
        out_shape=[jax.ShapeDtypeStruct((columns, width), F32)] * 2,
        in_specs=[anywhere, anywhere, vmem, vmem, vmem, vmem, smem, smem],
        out_specs=(vmem, vmem),
        scratch_shapes=[
            whole,
            pltpu.VMEM((tile_count * tile_obs, node_cols), BF16),
            pltpu.VMEM((CHIPS * PITCH, NODES), F32),
            parts,
            parts,
            parts,
            parts,
            pltpu.VMEM((1, TILES), F32),
            pltpu.VMEM((CHIPS, 1, TILES), F32),
            pltpu.VMEM((PARTS, CHIPS // 2, 1, NODES), F32),
            pltpu.VMEM((CHIPS, TILES, NODES), F32),
            pltpu.VMEM((2, SIDE, SIDE * SIDE, a_rows, grid_first), BF16),
            pltpu.VMEM((2, SIDE, NODES, NODES), BF16),
            pltpu.VMEM((LEVELS, GRID_A, GRID_A), BF16),
            field,
            field,
            pltpu.VMEM((2, LEVELS, GRID_A, NODES), F32),
            pltpu.VMEM((LEVELS * GRID_A, NODES), BF16),
            pltpu.VMEM((LEVELS, GRID_A, NODES), BF16),
            pltpu.VMEM((CHIPS, NODES), F32),
            pltpu.VMEM((CHIPS, 1, 2 * NODES), F32),
            pltpu.VMEM((CHIPS, 1, 2 * NODES), F32),
            pltpu.VMEM((2, 1, 2 * NODES), F32),
            pltpu.VMEM((2, 1, 2 * NODES), F32),
            pltpu.VMEM((2, 1, 2 * NODES), F32),
            pltpu.VMEM((2, CHIPS, 1, 2 * NODES), F32),
            pltpu.VMEM((2, CHIPS, 2 * NODES), F32),
            dma((2, PARTS)),
            dma((PARTS,)),
            dma((PARTS, GROUPS)),
            dma((PARTS,)),
            dma((PARTS, GROUPS)),
            dma,
            dma,
            dma,
            dma((2,)),
            dma((8,)),
            dma,
            dma((2,)),
            dma((2, LEVELS)),
            dma((2, LEVELS)),
            dma((2,)),
            dma((2,)),
        ],
        compiler_params=pltpu.CompilerParams(
            collective_id=0, has_side_effects=True, vmem_limit_bytes=60 << 20
        ),
        name="conjugate_gradients",
    )(
        rhs,
        tile_weights.reshape(tile_count * tile_obs, node_cols),
        tile_owner,
        tile_row.reshape(1, tile_count),
        axis_a.reshape(a_rows, grid_first),
        axis_b.reshape(node_cols, node_cols),
        coupling,
        noise,
    )


def solution(mesh):
    split = Mesh(mesh.devices.reshape(SIDE, SIDE, SIDE, 2), AXES)
    in_specs = (
        P(None, AXES),
        P(AXES, None, None),
        P(AXES, None),
        P(AXES),
        P(OBS, LVL, None),
        P(LVL, None, None),
        P(),
        P(),
    )
    out_specs = (P(None, AXES), P(None, AXES))
    return jax.shard_map(
        on_device, mesh=split, in_specs=in_specs, out_specs=out_specs, check_vma=False
    )
```

time: 168 us -> 145 us (0.86)
  Pallas kernels: 160 us -> 138 us
    pallas_call x1, Pallas kernels: 160 us -> 138 us  [on_device(): pl.pallas_call(kernel, out_shape=[jax.ShapeDtypeStruct((columns, width),...]
    unnamed x4 -> x5, local copies, waits for them, and re-layouts: 4.53 us -> 5.92 us
where the time goes in v3:
time: 145 us
  Pallas kernels  138 us (95%)
  local copies, waits for them, and re-layouts  5.92 us (4%)
    pallas_call x1, Pallas kernels, on_device(): pl.pallas_call(kernel, out_shape=[jax.ShapeDtypeStruct((columns, width),...  138 us
    unnamed x5, local copies, waits for them, and re-layouts  5.92 us

profile of v3, /device:TPU:1, one launch (start us, length us, event | category | flops | bytes accessed | tf_op | source)
XLA Modules:
  0.0 144.8 jit_solution(669861131862850218)
XLA Ops:
  0.6 1.4 copy.10.owner_ref
  2.0 138.3 %conjugate_gradients.1 = (f32[64,8192]{1,0:T(8,128)}, f32[64,8192]{1,0:T(8,128)}) custom-call(f32[64,8192]{1,0:T(8,128)} %rhs_hbm.1, bf16[8192,128]{1,0:T(8,128)(2,1)} %bitcast.4, s32[128,1]{1,0:T(8,128)} %copy.10.owner_ref, s32[1,128]{1,0:T(1,128)} %bitcast.7, bf16[8,128]{1,0:T(8,128)(2,1)} %bitcast.6, bf16[128,128]{1,0:T(8,128)(2,1)} %bitcast.5, ...), custom_call_target="tpu_custom_call" | custom-call | tf_op jit(solution)/shard_map/conjugate_gradients/pallas_call | solution.py:599
  140.3 0.0 copy-start
  140.3 3.2 %copy.13 = f32[64,8192]{1,0:T(8,128)} copy(f32[64,8192]{1,0:T(8,128)} %get-tuple-element.4) | data formatting | bytes 4194304
  143.5 0.0 copy-done
  143.5 1.3 copy.14
Async XLA Ops:
  140.3 3.2 %copy-start = (f32[64,8192]{1,0:T(8,128)S(1)}, f32[64,8192]{1,0:T(8,128)}, u32[]{:S(2)}) copy-start(f32[64,8192]{1,0:T(8,128)} %get-tuple-element.5) | copy-start | bytes 6291460

commit v4 on v3

--- a/solution.py
+++ b/solution.py
@@ -98,8 +98,9 @@
     z, y, x, core = (lax.axis_index(a) for a in AXES)
     me = (z * SIDE + y) * SIDE + x
     mine = z * SIDE + y
-    x_ahead = [lax.rem(x + d, SIDE) for d in range(SIDE)]
-    x_behind = [lax.rem(x + SIDE - d, SIDE) for d in range(SIDE)]
+    way = 1 - 2 * core
+    x_ahead = [lax.rem(x + SIDE + way * d, SIDE) for d in range(SIDE)]
+    x_behind = [lax.rem(x + SIDE - way * d, SIDE) for d in range(SIDE)]
 
     def ahead(q):
         places = []
@@ -108,8 +109,8 @@
             high = lax.div(q, 2)
             places.append(
                 (
-                    lax.rem(z + high + mid + low, SIDE),
-                    lax.rem(y + mid + 2 * low, SIDE),
+                    lax.rem(z + 12 + way * (high + mid + low), SIDE),
+                    lax.rem(y + 12 + way * (mid + 2 * low), SIDE),
                     x_ahead[low],
                 )
             )
@@ -122,8 +123,8 @@
             high = lax.div(q, 2)
             places.append(
                 (
-                    lax.rem(z + 12 - (high + mid + low), SIDE),
-                    lax.rem(y + 12 - (mid + 2 * low), SIDE),
+                    lax.rem(z + 12 - way * (high + mid + low), SIDE),
+                    lax.rem(y + 12 - way * (mid + 2 * low), SIDE),
                     x_behind[low],
                 )
             )
@@ -182,7 +183,10 @@
     def greet(place):
         pl.semaphore_signal(barrier, inc=1, device_id=place, device_id_type=MESH)
 
-    others(ahead, lambda k, place: greet((*place, core)))
+    around = [[lax.rem(v + d, SIDE) for d in range(SIDE)] for v in (z, y, x)]
+    for k in range(CHIPS - 1, 0, -1):
+        dz, dy, dx = k // (SIDE * SIDE), k // SIDE % SIDE, k % SIDE
+        greet((around[0][dz], around[1][dy], around[2][dx], core))
     greet((z, y, x, 1 - core))
 
     lane = lax.broadcasted_iota(jnp.int32, (CHIPS, WIDTH), 1)
@@ -194,8 +198,7 @@
 
     owner = owner_ref[...]
     base = (owner & (LEVELS - 1)) * GRID_A + (owner >> 3) * (GRID_A // 16)
-    base = jnp.transpose(jnp.broadcast_to(base.astype(F32), (TILES, NODES)))
-    place_out[...] = base[0:1, :] + row_ref[...].astype(F32)
+    place_out[...] = (base + row_ref[...]).astype(F32)
 
     def window(i):
         return pl.ds(pl.multiple_of(i * WIDTH, WIDTH), WIDTH)
@@ -245,7 +248,7 @@
     def folded(product):
         return product[:, :NODES] + product[:, NODES:]
 
-    def send_part(h):
+    def send_part(h, between=lambda: None):
         def pack(q):
             for j, place in enumerate(ahead(q)):
                 out_buf[h, q * GROUP + j] = turn[column(chip(place), h), :].astype(BF16)
@@ -259,6 +262,7 @@
 
         pack(0)
         pack(1)
+        between()
         local(out_buf.at[h, 0], in_buf.at[h, 0], in_sem.at[h, 0])
         start(0, 1)
 
@@ -438,10 +442,10 @@
         for load in loads[h]:
             load.wait()
         total = over_part(h, rhs_quads, total)
-        if h == 0:
-            pl.semaphore_wait(barrier, CHIPS)
-        send_part(h)
-        if h == 0:
+        if h:
+            send_part(h)
+        else:
+            send_part(h, lambda: pl.semaphore_wait(barrier, CHIPS))
             local(place_out, places.at[0], place_sem)
             local(axis_a_ref, all_a.at[core, x, mine], a_sem)
             local(axis_b_ref, all_b.at[core, x], b_sem)
@@ -556,22 +560,29 @@
     for h in range(1, PARTS):
         send_back(h, lambda: None)
 
-    def final_quads(quads, carry):
-        backs = gather_back(quads)
+    def ready_quads(quads, carry):
         alpha, beta = two(coef_rows[1, :, :NODES]), two(coef_rows[1, :, NODES:])
-        for i, back in zip(quads, backs):
+        for i in quads:
             start = rhs_ref[:, window(i)]
             left = residual_ref[:, window(i)]
             direction = left + beta * start
-            image = back + two(noise_rows[...]) * direction
-            solution_ref[:, window(i)] = coef_rows[0] * start + alpha * direction
-            residual_ref[:, window(i)] = left - alpha * image
+            step = alpha * direction
+            solution_ref[:, window(i)] = coef_rows[0] * start + step
+            residual_ref[:, window(i)] = left - two(noise_rows[...]) * step
+        return carry
+
+    def final_quads(quads, carry):
+        alpha = two(coef_rows[1, :, :NODES])
+        for i, back in zip(quads, gather_back(quads)):
+            residual_ref[:, window(i)] = residual_ref[:, window(i)] - alpha * back
         return carry
 
     for h in range(PARTS):
         receive_part(h)
         if h == 0:
             receive_coefs(1)
+            for p in range(PARTS):
+                over_part(p, ready_quads, 0)
         over_part(h, final_quads, 0)
 
     for h in range(PARTS):
@@ -589,7 +600,7 @@
     tile_count, tile_obs, node_cols = tile_weights.shape
     columns, width = rhs.shape
     a_rows, lvl_here, grid_first = axis_a.shape
-    anywhere = pl.BlockSpec(memory_space=pl.ANY)
+    anywhere = pl.BlockSpec(memory_space=pltpu.HBM)
     vmem = pl.BlockSpec(memory_space=pltpu.VMEM)
     smem = pl.BlockSpec(memory_space=pltpu.SMEM)
     dma = pltpu.SemaphoreType.DMA
@@ -598,7 +609,7 @@
     field = pltpu.VMEM((LEVELS, GRID_A, NODES), F32)
     return pl.pallas_call(
         kernel,
-        out_shape=[jax.ShapeDtypeStruct((columns, width), F32)] * 2,
+        out_shape=(whole, whole),
         in_specs=[anywhere, anywhere, vmem, vmem, vmem, vmem, smem, smem],
         out_specs=(vmem, vmem),
         scratch_shapes=[
@@ -647,13 +658,13 @@
             dma((2,)),
         ],
         compiler_params=pltpu.CompilerParams(
-            collective_id=0, has_side_effects=True, vmem_limit_bytes=60 << 20
+            collective_id=0, has_side_effects=True, vmem_limit_bytes=59 << 20
         ),
         name="conjugate_gradients",
     )(
         rhs,
         tile_weights.reshape(tile_count * tile_obs, node_cols),
-        tile_owner,
+        tile_owner.reshape(1, tile_count),
         tile_row.reshape(1, tile_count),
         axis_a.reshape(a_rows, grid_first),
         axis_b.reshape(node_cols, node_cols),

time: 145 us -> 138 us (0.952)
  Pallas kernels: 138 us -> 133 us
  local copies, waits for them, and re-layouts: 5.92 us -> 2.64 us
    pallas_call x1, Pallas kernels: 138 us -> 133 us  [on_device(): pl.pallas_call(kernel, out_shape=(whole, whole), in_specs=[anywhere, anyw...]
    unnamed x5 -> x2, local copies, waits for them, and re-layouts: 5.92 us -> 2.64 us
where the time goes in v4:
time: 138 us; the launch traced here: 137 us
  Pallas kernels  133 us (96%)
  local copies, waits for them, and re-layouts  2.64 us (2%)
    pallas_call x1, Pallas kernels, on_device(): pl.pallas_call(kernel, out_shape=(whole, whole), in_specs=[anywhere, anyw...  133 us

profile of v4, /device:TPU:1, one launch (start us, length us, event | category | flops | bytes accessed | tf_op | source)
XLA Modules:
  0.0 136.8 jit_solution(2553493641154284718)
XLA Ops:
  0.6 133.5 %conjugate_gradients.1 = (f32[64,8192]{1,0:T(8,128)S(1)}, f32[64,8192]{1,0:T(8,128)S(1)}) custom-call(f32[64,8192]{1,0:T(8,128)} %rhs_hbm.1, bf16[8192,128]{1,0:T(8,128)(2,1)} %bitcast.5, s32[1,128]{1,0:T(1,128)} %bitcast.8, s32[1,128]{1,0:T(1,128)} %bitcast.9, bf16[8,128]{1,0:T(8,128)(2,1)} %bitcast.7, bf16[128,128]{1,0:T(8,128)(2,1)} %bitcast.6, ...), custom_call_target="tpu_custom_call" | custom-call | tf_op jit(solution)/shard_map/conjugate_gradients/pallas_call | solution.py:610
  134.1 1.3 copy.12
  135.5 1.3 copy.13

commit v5 on v4

--- a/solution.py
+++ b/solution.py
@@ -105,7 +105,7 @@
     def ahead(q):
         places = []
         for j in range(GROUP):
-            low, mid = j % SIDE, 2 * lax.rem(q, 2) + j // SIDE
+            low, mid = (0, 1, 3, 2)[j % SIDE], 2 * lax.rem(q, 2) + j // SIDE
             high = lax.div(q, 2)
             places.append(
                 (
@@ -119,7 +119,7 @@
     def behind(q):
         places = []
         for j in range(GROUP):
-            low, mid = j % SIDE, 2 * lax.rem(q, 2) + j // SIDE
+            low, mid = (0, 1, 3, 2)[j % SIDE], 2 * lax.rem(q, 2) + j // SIDE
             high = lax.div(q, 2)
             places.append(
                 (
@@ -248,7 +248,7 @@
     def folded(product):
         return product[:, :NODES] + product[:, NODES:]
 
-    def send_part(h, between=lambda: None):
+    def send_part(h):
         def pack(q):
             for j, place in enumerate(ahead(q)):
                 out_buf[h, q * GROUP + j] = turn[column(chip(place), h), :].astype(BF16)
@@ -262,7 +262,6 @@
 
         pack(0)
         pack(1)
-        between()
         local(out_buf.at[h, 0], in_buf.at[h, 0], in_sem.at[h, 0])
         start(0, 1)
 
@@ -442,10 +441,10 @@
         for load in loads[h]:
             load.wait()
         total = over_part(h, rhs_quads, total)
-        if h:
-            send_part(h)
-        else:
-            send_part(h, lambda: pl.semaphore_wait(barrier, CHIPS))
+        if h == 0:
+            pl.semaphore_wait(barrier, CHIPS)
+        send_part(h)
+        if h == 0:
             local(place_out, places.at[0], place_sem)
             local(axis_a_ref, all_a.at[core, x, mine], a_sem)
             local(axis_b_ref, all_b.at[core, x], b_sem)

time: 138 us -> 137 us (level)
  no operation moved by 1% of the time
where the time goes in v5:
time: 137 us; the launch traced here: 136 us
  Pallas kernels  133 us (97%)
  local copies, waits for them, and re-layouts  2.64 us (2%)
    pallas_call x1, Pallas kernels, on_device(): pl.pallas_call(kernel, out_shape=(whole, whole), in_specs=[anywhere, anyw...  133 us

profile of v5, /device:TPU:1, one launch (start us, length us, event | category | flops | bytes accessed | tf_op | source)
XLA Modules:
  0.0 136.5 jit_solution(5698392083579166019)
XLA Ops:
  0.6 133.2 %conjugate_gradients.1 = (f32[64,8192]{1,0:T(8,128)S(1)}, f32[64,8192]{1,0:T(8,128)S(1)}) custom-call(f32[64,8192]{1,0:T(8,128)} %rhs_hbm.1, bf16[8192,128]{1,0:T(8,128)(2,1)} %bitcast.5, s32[1,128]{1,0:T(1,128)} %bitcast.8, s32[1,128]{1,0:T(1,128)} %bitcast.9, bf16[8,128]{1,0:T(8,128)(2,1)} %bitcast.7, bf16[128,128]{1,0:T(8,128)(2,1)} %bitcast.6, ...), custom_call_target="tpu_custom_call" | custom-call | tf_op jit(solution)/shard_map/conjugate_gradients/pallas_call | solution.py:609
  133.8 1.3 copy.12
  135.1 1.3 copy.13

commit v6 on v5

--- a/solution.py
+++ b/solution.py
@@ -66,6 +66,7 @@
     all_b,
     mat_a,
     acc,
+    low_acc,
     node_sums,
     partner_acc,
     grid_values,
@@ -303,9 +304,10 @@
             acc[...] += dot(chosen, parts).reshape(LEVELS, GRID_A, NODES)
 
     def exchange(step):
+        low_acc[...] = acc[...].astype(BF16)
         copies = [
             to_partner(
-                acc.at[l],
+                low_acc.at[l],
                 partner_acc.at[step, l],
                 acc_send_sem.at[step, l],
                 acc_sem.at[step, l],
@@ -334,7 +336,7 @@
             copy.wait()
         fields = []
         for l in range(LEVELS):
-            sums = acc[l] + partner_acc[step, l]
+            sums = low_acc[l].astype(F32) + partner_acc[step, l].astype(F32)
             if step:
                 sums = sums + beta * node_sums[l]
             node_sums[l] = sums
@@ -383,9 +385,9 @@
                 ).start()
 
         pick(0)
-        between()
         local(ret_buf.at[h, 0], got_buf.at[h, me], got_sem.at[h, 0])
         start(0, 1)
+        between()
         pick(1)
 
         @functools.partial(each, 2, GROUPS)
@@ -627,8 +629,9 @@
             pltpu.VMEM((2, SIDE, NODES, NODES), BF16),
             pltpu.VMEM((LEVELS, GRID_A, GRID_A), BF16),
             field,
+            pltpu.VMEM((LEVELS, GRID_A, NODES), BF16),
             field,
-            pltpu.VMEM((2, LEVELS, GRID_A, NODES), F32),
+            pltpu.VMEM((2, LEVELS, GRID_A, NODES), BF16),
             pltpu.VMEM((LEVELS * GRID_A, NODES), BF16),
             pltpu.VMEM((LEVELS, GRID_A, NODES), BF16),
             pltpu.VMEM((CHIPS, NODES), F32),

time: 137 us -> 136 us (level)
  no operation moved by 1% of the time
where the time goes in v6:
time: 136 us
  Pallas kernels  133 us (98%)
  local copies, waits for them, and re-layouts  2.64 us (2%)
    pallas_call x1, Pallas kernels, on_device(): pl.pallas_call(kernel, out_shape=(whole, whole), in_specs=[anywhere, anyw...  133 us

profile of v6, /device:TPU:1, one launch (start us, length us, event | category | flops | bytes accessed | tf_op | source)
XLA Modules:
  0.0 136.0 jit_solution(17799798708534765832)
XLA Ops:
  0.6 132.7 %conjugate_gradients.1 = (f32[64,8192]{1,0:T(8,128)S(1)}, f32[64,8192]{1,0:T(8,128)S(1)}) custom-call(f32[64,8192]{1,0:T(8,128)} %rhs_hbm.1, bf16[8192,128]{1,0:T(8,128)(2,1)} %bitcast.5, s32[1,128]{1,0:T(1,128)} %bitcast.8, s32[1,128]{1,0:T(1,128)} %bitcast.9, bf16[8,128]{1,0:T(8,128)(2,1)} %bitcast.7, bf16[128,128]{1,0:T(8,128)(2,1)} %bitcast.6, ...), custom_call_target="tpu_custom_call" | custom-call | tf_op jit(solution)/shard_map/conjugate_gradients/pallas_call | solution.py:611
  133.3 1.3 copy.12
  134.7 1.3 copy.13
